TPU v7x, 256 devices: a whole 4x4x8 slice. The times are simulated.
256 devices in a mesh: ang: 8 (over y, z_hi), tile: 32 (over z_lo, x, core).
Axes of the slice: x: 4, y: 4, z: 8 (z_hi: 2, z_lo: 4; z = z_hi * 4 + z_lo), core: 2. Of those that a mesh axis runs over, the one named last changes fastest.
Arguments:
- phase: float32 [4, 256, 256], P(None, 'tile'), may hold values from -1 to 1
- absorb: float32 [4, 256, 256], P(None, 'tile'), may hold values from 0 to 0.5
- tilts: int32 [512, 2], P(('ang', 'tile')), may hold values from -48 to 47
- windows: int32 [512], P(('ang', 'tile')), may hold values from 0 to 2
- live: int32 [512], P(('ang', 'tile')), may hold values 0 or 1
- measured: bfloat16 [2, 512, 256, 256], P(None, ('ang', 'tile')), may hold values from -24 to 24
Outputs:
- volume_out: float32 [2, 4, 256, 256], P(None, None, 'tile')
- gradient: float32 [2, 4, 256, 256], P(None, None, 'tile')
Inputs may be any that keep to these rules, and one draw needn't show every extreme that they name: Angle n passes slices windows[n] and windows[n] + 1. Angle slots with live 0 contribute nothing.
All inputs are finite; a program needn't handle non-finite values. No bound on the sum of `live` on one device may be relied on, other than what follows from the above.
Results may differ from a plain program's by a relative error of at most 0.0046.
Values may be sent and summed in bfloat16 or wider, within the bound.
No kernel may reach another device: no remote copies, remote signals or barrier semaphores. Data moves between devices by JAX's collectives and lax.ppermute only.
A program may use at most 64 MiB of HBM per device.

v0:
```python
import functools
import math

import jax
import jax.numpy as jnp
from jax import lax
from jax.sharding import PartitionSpec as P

TV_STEPS = 3


LAMBDA_TV = 0.25
TAU_DUAL = 0.5
EPS_HUBER = 0.1
STEP_SIZE = 0.5


def joined_along(tiles, dim):
    dims = list(tiles.shape[1:])
    dims[dim] *= tiles.shape[0]
    return jnp.moveaxis(tiles, 0, dim).reshape(dims)


def sent_to_all(value, axis):
    size = lax.axis_size(axis)
    return lax.all_to_all(
        jnp.broadcast_to(value[None], (size, *value.shape)), axis, 0, 0, tiled=True
    )


def collect(value, axis, dim):
    return joined_along(sent_to_all(value, axis), dim)


def cut_along(value, dim, size):
    before, after = (value.shape[:dim], value.shape[dim + 1 :])
    return jnp.moveaxis(value.reshape(*before, size, -1, *after), dim, 0)


def sum_at_owner(value, axis, dim):
    tiles = cut_along(value, dim, lax.axis_size(axis))
    arrived = lax.all_to_all(tiles, axis, split_axis=0, concat_axis=0, tiled=True)
    return arrived.sum(axis=0)


def over_copies(value, axis):
    everything = sent_to_all(value, axis)
    return jnp.sum(everything, axis=0)


def extended_2(value, sides, width):
    for axis, dim in sides:
        size, length = (lax.axis_size(axis), value.shape[dim])
        up = [(i, (i + 1) % size) for i in range(size - 1)]
        down = [(j, i) for i, j in up]
        last = lax.slice_in_dim(value, length - width, length, axis=dim)
        first = lax.slice_in_dim(value, 0, width, axis=dim)
        before = lax.ppermute(last, axis, up)
        after = lax.ppermute(first, axis, down)
        value = jnp.concatenate([before, value, after], axis=dim)
    return value


def circulant(column, length):
    tiled = jnp.tile(column, length + 1).reshape(length, length + 1)
    return tiled[:, 1:][:, ::-1]


def propagator(length):
    indices = jnp.arange(length, dtype=jnp.int32)
    frequency = jnp.where(indices < length // 2, indices, indices - length).astype(jnp.float32)
    kernel_phase = -(math.pi / length) * frequency * frequency
    phases = (indices[:, None] * indices[None, :] % length).astype(jnp.float32) * (
        2.0 * math.pi / length
    )
    cosines = jnp.cos(phases)
    sines = jnp.sin(phases)
    kernel_cos = jnp.cos(kernel_phase)
    kernel_sin = jnp.sin(kernel_phase)
    highest = lax.Precision.HIGHEST
    column_real = (
        jnp.dot(cosines, kernel_cos, precision=highest)
        - jnp.dot(sines, kernel_sin, precision=highest)
    ) / length
    column_imag = (
        jnp.dot(cosines, kernel_sin, precision=highest)
        + jnp.dot(sines, kernel_cos, precision=highest)
    ) / length
    real_part = circulant(column_real.astype(jnp.bfloat16), length)
    imag_part = circulant(column_imag.astype(jnp.bfloat16), length)
    forward_sweep = jnp.concatenate(
        [jnp.concatenate([real_part, -imag_part], 1), jnp.concatenate([imag_part, real_part], 1)], 0
    )
    backward_sweep = jnp.concatenate(
        [jnp.concatenate([real_part, imag_part], 1), jnp.concatenate([-imag_part, real_part], 1)], 0
    )
    return (forward_sweep, backward_sweep)


def apply_left(matrix, real, imag):
    length = real.shape[0]
    stacked = jnp.dot(
        matrix,
        jnp.concatenate([real, imag], 0).astype(jnp.bfloat16),
        preferred_element_type=jnp.float32,
    )
    return (stacked[:length], stacked[length:])


def apply_right(matrix, real, imag):
    length = real.shape[1]
    stacked = jnp.dot(
        jnp.concatenate([real, imag], 1).astype(jnp.bfloat16),
        matrix,
        preferred_element_type=jnp.float32,
    )
    return (stacked[:, :length], stacked[:, length:])


def incident(tilt_rowwise, tilt_column, length):
    indices = jnp.arange(length, dtype=jnp.int32)
    turns = (tilt_rowwise * indices[:, None] + tilt_column * indices[None, :]) % length
    phases = turns.astype(jnp.float32) * (2.0 * math.pi / length)
    return (jnp.cos(phases), jnp.sin(phases))


def single_angle(
    transmit_factor,
    forward_sweep,
    backward_sweep,
    tilt_rowwise,
    tilt_column,
    start_offset,
    observed_real,
    observed_imag,
):
    length = transmit_factor.shape[2]
    block = lax.dynamic_slice_in_dim(transmit_factor, start_offset, 2, 1).astype(jnp.float32)
    first_real, first_imag = (block[0, 0], block[1, 0])
    second_real, second_imag = (block[0, 1], block[1, 1])
    wave_real, wave_imag = incident(tilt_rowwise, tilt_column, length)
    enter_real = wave_real * first_real - wave_imag * first_imag
    enter_imag = wave_real * first_imag + wave_imag * first_real
    mid_real, mid_imag = apply_left(forward_sweep, enter_real, enter_imag)
    prop_real, prop_imag = apply_right(backward_sweep, mid_real, mid_imag)
    outgoing_real = prop_real * second_real - prop_imag * second_imag
    outgoing_imag = prop_real * second_imag + prop_imag * second_real
    residual_real = outgoing_real - observed_real.astype(jnp.float32)
    residual_imag = outgoing_imag - observed_imag.astype(jnp.float32)
    phase_two = outgoing_real * residual_imag - outgoing_imag * residual_real
    absorb_two = -(outgoing_real * residual_real + outgoing_imag * residual_imag)
    adj_real = second_real * residual_real + second_imag * residual_imag
    adj_imag = second_real * residual_imag - second_imag * residual_real
    half_real, half_imag = apply_left(backward_sweep, adj_real, adj_imag)
    back_real, back_imag = apply_right(forward_sweep, half_real, half_imag)
    phase_one = enter_real * back_imag - enter_imag * back_real
    absorb_one = -(enter_real * back_real + enter_imag * back_imag)
    return jnp.stack([jnp.stack([phase_one, phase_two]), jnp.stack([absorb_one, absorb_two])])


def divergence(dual_rows, dual_cols, above):
    shifted = jnp.concatenate([above, dual_rows[:, :, :-1, :]], 2)
    left = jnp.pad(dual_cols[..., :-1], ((0, 0), (0, 0), (0, 0), (1, 0)))
    return dual_rows - shifted + dual_cols - left


def slopes(primal, below, keep_rows, inside):
    shifted = jnp.concatenate([primal[:, :, 1:, :], below], 2)
    diff_rows = (shifted - primal) * keep_rows
    diff_cols = (
        jnp.pad(primal[..., 1:] - primal[..., :-1], ((0, 0), (0, 0), (0, 0), (0, 1))) * inside
    )
    return (diff_rows, diff_cols)


def dual_update(dual_rows, dual_cols, diff_rows, diff_cols):
    new_rows = (dual_rows + TAU_DUAL * diff_rows) / (1.0 + TAU_DUAL * EPS_HUBER)
    new_cols = (dual_cols + TAU_DUAL * diff_cols) / (1.0 + TAU_DUAL * EPS_HUBER)
    scale = jnp.maximum(1.0, jnp.sqrt(new_rows * new_rows + new_cols * new_cols))
    return (new_rows / scale, new_cols / scale)


def row_masks(first_global, count, length):
    global_rows = first_global + jnp.arange(count, dtype=jnp.int32)
    inside = ((global_rows >= 0) & (global_rows < length)).astype(jnp.float32)
    keep_rows = inside * (global_rows < length - 1).astype(jnp.float32)
    return (keep_rows[:, None], inside[:, None])


def on_device(phase, absorb, tilts, windows, live, measured):
    slots = tilts.shape[0]
    strip = phase.shape[1]
    length = phase.shape[2]
    forward_sweep, backward_sweep = propagator(length)
    decay = jnp.exp(-absorb)
    local_trans = jnp.stack([decay * jnp.cos(phase), decay * jnp.sin(phase)]).astype(jnp.bfloat16)
    transmit_factor = collect(local_trans, "tile", 2)
    depth = transmit_factor.shape[1]

    def accumulate(slot, total):
        term_list = single_angle(
            transmit_factor,
            forward_sweep,
            backward_sweep,
            tilts[slot, 0],
            tilts[slot, 1],
            windows[slot],
            measured[0, slot],
            measured[1, slot],
        )
        begin = windows[slot]
        current = lax.dynamic_slice_in_dim(total, begin, 2, 1)
        return lax.dynamic_update_slice_in_dim(total, current + term_list, begin, 1)

    def keep_total(total):
        return total

    total = jnp.zeros((2, depth, length, length), jnp.float32)
    for slot in range(slots):
        total = lax.cond(live[slot] > 0, functools.partial(accumulate, slot), keep_total, total)
    owned = sum_at_owner(total, "tile", 2)
    summed = over_copies(owned, "ang")
    all_slots = slots * lax.axis_size("ang") * lax.axis_size("tile")
    gradient = summed * (1.0 / math.sqrt(all_slots))
    volume = jnp.stack([phase, absorb]) - STEP_SIZE * gradient
    first_row = lax.axis_index("tile") * strip
    extended = extended_2(volume, (("tile", 2),), TV_STEPS)
    count = strip + 2 * TV_STEPS
    keep_rows, inside = row_masks(first_row - TV_STEPS, count, length)
    zero_row = jnp.zeros((2, depth, 1, length), jnp.float32)
    dual_rows = jnp.zeros_like(extended)
    dual_cols = jnp.zeros_like(extended)
    for repeat in range(TV_STEPS):
        primal = extended + LAMBDA_TV * divergence(dual_rows, dual_cols, zero_row)
        diff_rows, diff_cols = slopes(primal, zero_row, keep_rows, inside)
        dual_rows, dual_cols = dual_update(dual_rows, dual_cols, diff_rows, diff_cols)
    wide_out = extended + LAMBDA_TV * divergence(dual_rows, dual_cols, zero_row)
    volume_out = wide_out[:, :, TV_STEPS : TV_STEPS + strip, :]
    return (volume_out, gradient)


def solution(mesh):
    placed = (
        P(None, "tile", None),
        P(None, "tile", None),
        P(("ang", "tile"), None),
        P(("ang", "tile")),
        P(("ang", "tile")),
        P(None, ("ang", "tile"), None, None),
    )
    return jax.shard_map(
        on_device,
        mesh=mesh,
        in_specs=placed,
        out_specs=(P(None, None, "tile", None), P(None, None, "tile", None)),
        check_vma=False,
    )
```

profile of v0, /device:TPU:7, one launch (start us, length us, event | category | flops | bytes accessed | tf_op | source)
XLA Modules:
  0.0 155.3 jit_solution(3418324022862120634)
XLA Ops:
  0.6 0.9 fusion.76
  1.6 1.1 broadcast_in_dim.9
  2.7 9.3 %all-to-all-start = ((bf16[32,2,4,8,256]{4,3,2,1,0:T(8,128)(2,1)}), bf16[32,2,4,8,256]{4,3,2,1,0:T(8,128)(2,1)S(1)}, u32[]{:S(2)}, u32[]{:S(2)}) async-start(bf16[32,2,4,8,256]{4,3,2,1,0:T(8,128)(2,1)} %broadcast_in_dim.9), calls=%async_computation | async-start | bytes 2097152 | tf_op jit(solution)/shard_map/all_to_all | solution.py:26
  12.1 1.2 fusion.67
  13.3 1.3 fusion.71
  15.8 1.2 fusion.69
  17.0 1.3 fusion.73
  21.4 16.7 %all-to-all-done = bf16[32,2,4,8,256]{4,3,2,1,0:T(8,128)(2,1)S(1)} async-done(((bf16[32,2,4,8,256]{4,3,2,1,0:T(8,128)(2,1)}), bf16[32,2,4,8,256]{4,3,2,1,0:T(8,128)(2,1)S(1)}, u32[]{:S(2)}, u32[]{:S(2)}) %all-to-all-start) | async-done | bytes 1048608 | tf_op jit(solution)/shard_map/all_to_all | solution.py:26
  38.2 7.9 %conditional.2 = (f32[2,4,256,256]{3,2,1,0:T(8,128)}) conditional(s32[]{:T(128)} %bitcast.37, () %tuple.20, (s32[2,2]{1,0:T(2,128)S(1)}, s32[2]{0:T(128)S(1)}, bf16[2,4,256,256]{3,2,1,0:T(8,128)(2,1)S(1)}, bf16[512,512]{1,0:T(8,128)(2,1)S(1)}, bf16[512,512]{1,0:T(8,128)(2,1)S(1)}, /*index=5*/bf16[2,2,256,256]{3,2,1,0:T(8,128)(2,1)}) %tuple.67), branch_computations={%region_0.1_spmd, %region_1.2_spmd} | conditional | flops 543818240 | bytes 22548586 | solution.py:220
  39.1 1.3 iota_multiply_fusion
  40.4 1.3 fusion.97
  43.6 1.5 broadcast_in_dim.1
  45.1 1.0 maximum_dynamic-update-slice_fusion
  46.1 10.1 %conditional.3 = (f32[2,4,256,256]{3,2,1,0:T(8,128)}) conditional(s32[]{:T(128)} %bitcast.36, f32[2,4,256,256]{3,2,1,0:T(8,128)} %get-tuple-element.110, (s32[2]{0:T(128)S(1)}, f32[2,4,256,256]{3,2,1,0:T(8,128)}, s32[2,2]{1,0:T(2,128)S(1)}, bf16[2,4,256,256]{3,2,1,0:T(8,128)(2,1)S(1)}, bf16[512,512]{1,0:T(8,128)(2,1)S(1)}, ...), branch_computations={%region_2.3_spmd, %region_3.4_spmd} | conditional | flops 544080384 | bytes 21500014 | solution.py:220
  49.4 1.3 iota_multiply_fusion.2
  50.8 1.3 fusion.99
  53.9 2.3 %fusion.27 = f32[2,4,256,256]{3,2,1,0:T(8,128)} fusion(f32[2,4,256,256]{3,2,1,0:T(8,128)} %get-tuple-element.39, s32[]{:T(128)S(6)} %select_n.30, f32[1,2,256,256]{3,2,1,0:T(8,128)S(1)} %maximum_bitcast_fusion.3, f32[1,2,256,256]{3,2,1,0:T(8,128)S(1)} %maximum_bitcast_fusion.2), kind=kLoop, calls=%fused_computation.59 | loop fusion | flops 524288 | bytes 3145732 | tf_op jit(solution)/shard_map/cond/branch_1_fun/dynamic_update_slice | solution.py:213
  56.2 1.8 %copy.11 = f32[32,2,4,8,256]{4,3,2,1,0:T(8,128)S(1)} copy(f32[32,2,4,8,256]{4,3,0,2,1:T(8,128)} %bitcast.52) | data formatting | bytes 4194304 | tf_op jit(solution)/shard_map/transpose | solution.py:37
  58.1 53.8 %all_to_all.15 = f32[32,2,4,8,256]{4,3,2,1,0:T(8,128)S(1)} all-to-all(f32[32,2,4,8,256]{4,3,2,1,0:T(8,128)S(1)} %copy.11), channel_id=1, replica_groups=mesh['ang'=8,'tile'=32] {'tile'}, dimensions={0} | all-to-all | bytes 4194304 | tf_op jit(solution)/shard_map/all_to_all | solution.py:42
  112.9 8.3 %all-to-all-start.2 = ((f32[8,2,4,8,256]{4,3,2,1,0:T(8,128)}), f32[8,2,4,8,256]{4,3,2,1,0:T(8,128)S(1)}, u32[]{:S(2)}, u32[]{:S(2)}) async-start(f32[8,2,4,8,256]{4,3,2,1,0:T(8,128)} %broadcast_in_dim.10), calls=%async_computation.2 | async-start | bytes 1048576 | tf_op jit(solution)/shard_map/all_to_all | solution.py:26
  121.3 15.9 %all-to-all-done.2 = f32[8,2,4,8,256]{4,3,2,1,0:T(8,128)S(1)} async-done(((f32[8,2,4,8,256]{4,3,2,1,0:T(8,128)}), f32[8,2,4,8,256]{4,3,2,1,0:T(8,128)S(1)}, u32[]{:S(2)}, u32[]{:S(2)}) %all-to-all-start.2) | async-done | bytes 524320 | tf_op jit(solution)/shard_map/all_to_all | solution.py:26
  137.9 7.9 %collective-permute-start = (f32[2,4,3,256]{3,2,1,0:T(4,128)S(1)}, f32[2,4,3,256]{3,2,1,0:T(4,128)S(1)}, u32[]{:S(2)}, u32[]{:S(2)}) collective-permute-start(f32[2,4,3,256]{3,2,1,0:T(4,128)S(1)} %get-tuple-element.104), channel_id=1, source_target_pairs={{0,1},{1,2},{2,3},{3,4},{4,5},{5,6},{6,7},{7,8},{8,9},{9,10},{10,1... | collective-permute-start | bytes 73736 | tf_op jit(solution)/shard_map/ppermute | solution.py:58
  145.8 1.9 %collective-permute-start.1 = (f32[2,4,3,256]{3,2,1,0:T(4,128)S(1)}, f32[2,4,3,256]{3,2,1,0:T(4,128)S(1)}, u32[]{:S(2)}, u32[]{:S(2)}) collective-permute-start(f32[2,4,3,256]{3,2,1,0:T(4,128)S(1)} %get-tuple-element.105), channel_id=1, source_target_pairs={{1,0},{2,1},{3,2},{4,3},{5,4},{6,5},{7,6},{8,7},{9,8},{10,9},{11,1... | collective-permute-start | bytes 73736 | tf_op jit(solution)/shard_map/ppermute | solution.py:59
  147.7 5.4 %collective-permute-done.1 = f32[2,4,3,256]{3,2,1,0:T(4,128)S(1)} collective-permute-done((f32[2,4,3,256]{3,2,1,0:T(4,128)S(1)}, f32[2,4,3,256]{3,2,1,0:T(4,128)S(1)}, u32[]{:S(2)}, u32[]{:S(2)}) %collective-permute-start.1) | collective-permute-done | bytes 24608 | tf_op jit(solution)/shard_map/ppermute | solution.py:59
  (83 shorter events, 12.5 us)
Async XLA Ops:
  2.7 35.5 %all-to-all-start = ((bf16[32,2,4,8,256]{4,3,2,1,0:T(8,128)(2,1)}), bf16[32,2,4,8,256]{4,3,2,1,0:T(8,128)(2,1)S(1)}, u32[]{:S(2)}, u32[]{:S(2)}) async-start(bf16[32,2,4,8,256]{4,3,2,1,0:T(8,128)(2,1)} %broadcast_in_dim.9), calls=%async_computation | async-start | bytes 2097152 | tf_op jit(solution)/shard_map/all_to_all | solution.py:26
  14.7 4.7 %copy-start.5 = (s32[2]{0:T(128)S(1)}, s32[2]{0:T(128)}, u32[]{:S(2)}) copy-start(s32[2]{0:T(128)} %param.14) | copy-start | bytes 28
  18.8 19.4 %copy-start.4 = (s32[2,2]{1,0:T(2,128)S(1)}, s32[2,2]{1,0:T(2,128)}, u32[]{:S(2)}) copy-start(s32[2,2]{1,0:T(2,128)} %param.12) | copy-start | bytes 52
  18.8 19.4 %copy-start.6 = (s32[2]{0:T(128)S(1)}, s32[2]{0:T(128)}, u32[]{:S(2)}) copy-start(s32[2]{0:T(128)} %param.13) | copy-start | bytes 28
  40.4 2.0 %copy-start = (bf16[2,2,256,256]{3,2,1,0:T(8,128)(2,1)S(1)}, bf16[2,2,256,256]{3,2,1,0:T(8,128)(2,1)}, u32[]{:S(2)}) copy-start(bf16[2,2,256,256]{3,2,1,0:T(8,128)(2,1)} %get-tuple-element.38) | copy-start | bytes 1572868 | tf_op jit(solution)/shard_map/cond
  50.8 2.0 %copy-start.1 = (bf16[2,2,256,256]{3,2,1,0:T(8,128)(2,1)S(1)}, bf16[2,2,256,256]{3,2,1,0:T(8,128)(2,1)}, u32[]{:S(2)}) copy-start(bf16[2,2,256,256]{3,2,1,0:T(8,128)(2,1)} %get-tuple-element.45) | copy-start | bytes 1572868 | tf_op jit(solution)/shard_map/cond
  111.9 25.3 %copy-start.2 = (f32[4,8,256]{2,1,0:T(8,128)S(1)}, f32[4,8,256]{2,1,0:T(8,128)}, u32[]{:S(2)}) copy-start(f32[4,8,256]{2,1,0:T(8,128)} %param.10) | copy-start | bytes 98308
  111.9 25.3 %copy-start.3 = (f32[4,8,256]{2,1,0:T(8,128)S(1)}, f32[4,8,256]{2,1,0:T(8,128)}, u32[]{:S(2)}) copy-start(f32[4,8,256]{2,1,0:T(8,128)} %param.11) | copy-start | bytes 98308
  112.9 24.3 %all-to-all-start.2 = ((f32[8,2,4,8,256]{4,3,2,1,0:T(8,128)}), f32[8,2,4,8,256]{4,3,2,1,0:T(8,128)S(1)}, u32[]{:S(2)}, u32[]{:S(2)}) async-start(f32[8,2,4,8,256]{4,3,2,1,0:T(8,128)} %broadcast_in_dim.10), calls=%async_computation.2 | async-start | bytes 1048576 | tf_op jit(solution)/shard_map/all_to_all | solution.py:26
  137.9 9.8 %collective-permute-start = (f32[2,4,3,256]{3,2,1,0:T(4,128)S(1)}, f32[2,4,3,256]{3,2,1,0:T(4,128)S(1)}, u32[]{:S(2)}, u32[]{:S(2)}) collective-permute-start(f32[2,4,3,256]{3,2,1,0:T(4,128)S(1)} %get-tuple-element.104), channel_id=1, source_target_pairs={{0,1},{1,2},{2,3},{3,4},{4,5},{5,6},{6,7},{7,8},{8,9},{9,10},{10,1... | collective-permute-start | bytes 73736 | tf_op jit(solution)/shard_map/ppermute | solution.py:58
  145.8 7.3 %collective-permute-start.1 = (f32[2,4,3,256]{3,2,1,0:T(4,128)S(1)}, f32[2,4,3,256]{3,2,1,0:T(4,128)S(1)}, u32[]{:S(2)}, u32[]{:S(2)}) collective-permute-start(f32[2,4,3,256]{3,2,1,0:T(4,128)S(1)} %get-tuple-element.105), channel_id=1, source_target_pairs={{1,0},{2,1},{3,2},{4,3},{5,4},{6,5},{7,6},{8,7},{9,8},{10,9},{11,1... | collective-permute-start | bytes 73736 | tf_op jit(solution)/shard_map/ppermute | solution.py:59
where the time goes:
time: 156 us; the launch traced here: 155 us
  blocking collectives  53.8 us (34%)
  waiting for transfers between devices  38 us (24%)
  starting transfers between devices  27.4 us (18%)
  other arithmetic  13.8 us (9%)
  local copies, waits for them, and re-layouts  10 us (6%)
  matrix products  7.7 us (5%)
  loops' own time  2.31 us (1%)
  between operations  2.23 us (1%)
    all_to_all x1, blocking collectives, sum_at_owner(): lax.all_to_all(tiles, axis, split_axis=0, concat_axis=0, tiled=True)  53.8 us
    all_to_all x2, waiting for transfers between devices, sent_to_all(): lax.all_to_all(jnp.broadcast_to(value[None], (size, *value.shape)), axis,...  32.6 us
    all_to_all x2, starting transfers between devices, sent_to_all(): lax.all_to_all(jnp.broadcast_to(value[None], (size, *value.shape)), axis,...  17.6 us
    ppermute x1, starting transfers between devices, extended_2(): before = lax.ppermute(last, axis, up)  7.88 us
    ppermute x1, waiting for transfers between devices, extended_2(): after = lax.ppermute(first, axis, down)  5.39 us
    dynamic_update_slice x2, other arithmetic, accumulate(): return lax.dynamic_update_slice_in_dim(total, current + term_list, begin, 1)  3.34 us
  transfers between devices with their start and end apart: 4, of which 3 were waited for; matrix products, arithmetic and copies ran while one was open for 5% of the time, Pallas kernels for 0%

commit v1 on v0

v1 whole, which is shorter than its diff:
```python
import math

import jax
import jax.numpy as jnp
from jax import lax
from jax.experimental import pallas as pl
from jax.experimental.pallas import tpu as pltpu
from jax.sharding import Mesh
from jax.sharding import PartitionSpec as P

TV_STEPS = 3


LAMBDA_TV = 0.25
TAU_DUAL = 0.5
EPS_HUBER = 0.1
STEP_SIZE = 0.5

AXES = ("y", "zh", "zl", "x", "c")
SIZES = (4, 2, 4, 4, 2)
ANG = ("y", "zh")
TILE = ("zl", "x", "c")
CHIPS = ("zl", "x")


def swap_cores(value):
    return lax.ppermute(value, "c", [(0, 1), (1, 0)])


def exchange(value, axes):
    return lax.all_to_all(value, axes, split_axis=0, concat_axis=0, tiled=True)


def propagator(length):
    indices = jnp.arange(length, dtype=jnp.int32)
    gaps = indices[:, None] - indices[None, :]
    turns = (gaps * gaps) % (2 * length)
    phases = turns.astype(jnp.float32) * (math.pi / length) - math.pi / 4
    scale = 1.0 / math.sqrt(length)
    real_part = (jnp.cos(phases) * scale).astype(jnp.bfloat16)
    imag_part = (jnp.sin(phases) * scale).astype(jnp.bfloat16)
    forward_sweep = jnp.concatenate(
        [jnp.concatenate([real_part, -imag_part], 1), jnp.concatenate([imag_part, real_part], 1)], 0
    )
    backward_sweep = jnp.concatenate(
        [jnp.concatenate([real_part, imag_part], 1), jnp.concatenate([-imag_part, real_part], 1)], 0
    )
    return (forward_sweep, backward_sweep)


def angles_kernel(
    numbers, own, other, forward, backward, measured, out, first, wide, tall, acc
):
    length = acc.shape[2]
    slots = measured.shape[1]
    core = numbers[0]
    mine_first = core == 0

    def slice_plane(part, level):
        mine = own[:, part, level].astype(jnp.float32)
        theirs = other[:, part, level].astype(jnp.float32)
        upper = jnp.where(mine_first, mine, theirs)
        lower = jnp.where(mine_first, theirs, mine)
        return jnp.stack([upper, lower], 1).reshape(length, length)

    def factor(tilt, axis):
        shape = (length, 1) if axis == 0 else (1, length)
        index = lax.broadcasted_iota(jnp.int32, shape, axis)
        turns = (tilt * index) & (length - 1)
        phases = turns.astype(jnp.float32) * (2.0 * math.pi / length)
        return jnp.cos(phases), jnp.sin(phases)

    def span(slot):
        return slice(slot * length, (slot + 1) * length)

    acc[...] = jnp.zeros_like(acc)
    for slot in range(slots):
        level = numbers[3 + 4 * slot]
        row_cos, row_sin = factor(numbers[1 + 4 * slot], 0)
        col_cos, col_sin = factor(numbers[2 + 4 * slot], 1)
        wave_real = row_cos * col_cos - row_sin * col_sin
        wave_imag = row_cos * col_sin + row_sin * col_cos
        first_real = slice_plane(0, level)
        first_imag = slice_plane(1, level)
        enter_real = wave_real * first_real - wave_imag * first_imag
        enter_imag = wave_real * first_imag + wave_imag * first_real
        first[0, slot] = enter_real
        first[1, slot] = enter_imag
        tall[:length, span(slot)] = enter_real.astype(jnp.bfloat16)
        tall[length:, span(slot)] = enter_imag.astype(jnp.bfloat16)
    middle = jnp.dot(forward[...], tall[...], preferred_element_type=jnp.float32)
    for slot in range(slots):
        wide[span(slot), :length] = middle[:length, span(slot)].astype(jnp.bfloat16)
        wide[span(slot), length:] = middle[length:, span(slot)].astype(jnp.bfloat16)
    spread = jnp.dot(wide[...], backward[...], preferred_element_type=jnp.float32)
    for slot in range(slots):
        level = numbers[3 + 4 * slot]
        active = numbers[4 + 4 * slot].astype(jnp.float32)
        prop_real = spread[span(slot), :length]
        prop_imag = spread[span(slot), length:]
        second_real = slice_plane(0, level + 1)
        second_imag = slice_plane(1, level + 1)
        outgoing_real = prop_real * second_real - prop_imag * second_imag
        outgoing_imag = prop_real * second_imag + prop_imag * second_real
        residual_real = (outgoing_real - measured[0, slot].astype(jnp.float32)) * active
        residual_imag = (outgoing_imag - measured[1, slot].astype(jnp.float32)) * active
        acc[0, level + 1] += outgoing_real * residual_imag - outgoing_imag * residual_real
        acc[1, level + 1] -= outgoing_real * residual_real + outgoing_imag * residual_imag
        adj_real = second_real * residual_real + second_imag * residual_imag
        adj_imag = second_real * residual_imag - second_imag * residual_real
        tall[:length, span(slot)] = adj_real.astype(jnp.bfloat16)
        tall[length:, span(slot)] = adj_imag.astype(jnp.bfloat16)
    half = jnp.dot(backward[...], tall[...], preferred_element_type=jnp.float32)
    for slot in range(slots):
        wide[span(slot), :length] = half[:length, span(slot)].astype(jnp.bfloat16)
        wide[span(slot), length:] = half[length:, span(slot)].astype(jnp.bfloat16)
    back = jnp.dot(wide[...], forward[...], preferred_element_type=jnp.float32)
    for slot in range(slots):
        level = numbers[3 + 4 * slot]
        enter_real = first[0, slot]
        enter_imag = first[1, slot]
        back_real = back[span(slot), :length]
        back_imag = back[span(slot), length:]
        acc[0, level] += enter_real * back_imag - enter_imag * back_real
        acc[1, level] -= enter_real * back_real + enter_imag * back_imag
    columns = out.shape[2]
    blocks = out.shape[3]
    rows = out.shape[4]
    for component in range(2):
        place = jnp.where(core == component, 0, 1)
        for level in range(acc.shape[1]):
            plane = acc[component, level].astype(jnp.bfloat16)
            plane = plane.reshape(blocks, columns, rows, length)
            for column in range(columns):
                out[place, level, column] = plane[:, column]


def angles(numbers, own, other, forward, backward, measured):
    length = measured.shape[-1]
    depth = own.shape[2]
    slots = measured.shape[1]
    strips = own.shape[0]
    zl, x = SIZES[2], SIZES[3]
    vmem = pl.BlockSpec(memory_space=pltpu.VMEM)
    return pl.pallas_call(
        angles_kernel,
        out_shape=jax.ShapeDtypeStruct((2, depth, x, zl, length // strips, length), jnp.bfloat16),
        in_specs=[pl.BlockSpec(memory_space=pltpu.SMEM)] + [vmem] * 5,
        out_specs=vmem,
        scratch_shapes=[
            pltpu.VMEM((2, slots, length, length), jnp.float32),
            pltpu.VMEM((slots * length, 2 * length), jnp.bfloat16),
            pltpu.VMEM((2 * length, slots * length), jnp.bfloat16),
            pltpu.VMEM((2, depth, length, length), jnp.float32),
        ],
        name="angles",
    )(numbers, own, other, forward, backward, measured)


def divergence(dual_rows, dual_cols, above):
    shifted = jnp.concatenate([above, dual_rows[:, :, :-1, :]], 2)
    left = jnp.pad(dual_cols[..., :-1], ((0, 0), (0, 0), (0, 0), (1, 0)))
    return dual_rows - shifted + dual_cols - left


def slopes(primal, below, keep_rows, inside):
    shifted = jnp.concatenate([primal[:, :, 1:, :], below], 2)
    diff_rows = (shifted - primal) * keep_rows
    diff_cols = (
        jnp.pad(primal[..., 1:] - primal[..., :-1], ((0, 0), (0, 0), (0, 0), (0, 1))) * inside
    )
    return (diff_rows, diff_cols)


def dual_update(dual_rows, dual_cols, diff_rows, diff_cols):
    new_rows = (dual_rows + TAU_DUAL * diff_rows) / (1.0 + TAU_DUAL * EPS_HUBER)
    new_cols = (dual_cols + TAU_DUAL * diff_cols) / (1.0 + TAU_DUAL * EPS_HUBER)
    scale = jnp.maximum(1.0, jnp.sqrt(new_rows * new_rows + new_cols * new_cols))
    return (new_rows / scale, new_cols / scale)


def row_masks(first_global, count, length):
    global_rows = first_global + jnp.arange(count, dtype=jnp.int32)
    inside = ((global_rows >= 0) & (global_rows < length)).astype(jnp.float32)
    keep_rows = inside * (global_rows < length - 1).astype(jnp.float32)
    return (keep_rows[:, None], inside[:, None])


def on_device(phase, absorb, tilts, windows, live, measured):
    slots = tilts.shape[0]
    depth, strip, length = phase.shape
    chips = length // (2 * strip)
    core = lax.axis_index("c")

    decay = jnp.exp(-absorb)
    local_trans = jnp.stack([decay * jnp.cos(phase), decay * jnp.sin(phase)]).astype(jnp.bfloat16)
    own = exchange(jnp.broadcast_to(local_trans[None], (chips, *local_trans.shape)), CHIPS)
    other = swap_cores(own)
    params = jnp.stack([phase, absorb])
    partner_params = swap_cores(params)

    forward_sweep, backward_sweep = propagator(length)
    numbers = jnp.concatenate(
        [core[None].astype(jnp.int32), jnp.concatenate([tilts, windows[:, None], live[:, None]], 1).reshape(-1)]
    )
    halves = angles(numbers, own, other, forward_sweep, backward_sweep, measured)

    pair = halves[0].astype(jnp.float32) + swap_cores(halves[1]).astype(jnp.float32)
    y, x = SIZES[0], SIZES[3]
    pair = pair.astype(jnp.bfloat16).reshape(y * x, -1, 2 * strip, length)
    plane = exchange(pair, ("y", "x")).astype(jnp.float32).sum(0).astype(jnp.bfloat16)
    copies = SIZES[0] * SIZES[1]
    sent = jnp.broadcast_to(plane[None], (copies, *plane.shape)).reshape(-1, *plane.shape[1:])
    column = exchange(sent, ("y", "zh", "zl")).astype(jnp.float32)
    column = column.reshape(depth, -1, 2 * strip, length).sum(1)
    all_slots = slots * math.prod(SIZES)
    mine = column * (1.0 / math.sqrt(all_slots))
    theirs = swap_cores(mine)
    both = jnp.stack([jnp.where(core == 0, mine, theirs), jnp.where(core == 0, theirs, mine)])
    upper, lower = both[:, :, :strip], both[:, :, strip:]
    gradient = jnp.where(core == 0, upper, lower)
    partner_gradient = jnp.where(core == 0, lower, upper)
    volume = params - STEP_SIZE * gradient
    partner_volume = partner_params - STEP_SIZE * partner_gradient

    last = volume[:, :, strip - TV_STEPS :]
    head = volume[:, :, :TV_STEPS]
    tiles = SIZES[2] * SIZES[3] * SIZES[4]
    borders = [(i, i + 1) for i in range(1, tiles - 1, 2)]
    borders = borders + [(j, i) for i, j in borders]
    far = lax.ppermute(jnp.where(core == 0, head, last), TILE, borders)
    before = jnp.where(core == 0, far, partner_volume[:, :, strip - TV_STEPS :])
    after = jnp.where(core == 0, partner_volume[:, :, :TV_STEPS], far)
    extended = jnp.concatenate([before, volume, after], 2)

    first_row = lax.axis_index(TILE) * strip
    count = strip + 2 * TV_STEPS
    keep_rows, inside = row_masks(first_row - TV_STEPS, count, length)
    zero_row = jnp.zeros((2, depth, 1, length), jnp.float32)
    dual_rows = jnp.zeros_like(extended)
    dual_cols = jnp.zeros_like(extended)
    for repeat in range(TV_STEPS):
        primal = extended + LAMBDA_TV * divergence(dual_rows, dual_cols, zero_row)
        diff_rows, diff_cols = slopes(primal, zero_row, keep_rows, inside)
        dual_rows, dual_cols = dual_update(dual_rows, dual_cols, diff_rows, diff_cols)
    wide_out = extended + LAMBDA_TV * divergence(dual_rows, dual_cols, zero_row)
    volume_out = wide_out[:, :, TV_STEPS : TV_STEPS + strip, :]
    return (volume_out, gradient)


def solution(mesh):
    fine = Mesh(mesh.devices.reshape(SIZES), AXES)
    slots = (*ANG, *TILE)
    placed = (
        P(None, TILE, None),
        P(None, TILE, None),
        P(slots, None),
        P(slots),
        P(slots),
        P(None, slots, None, None),
    )
    return jax.shard_map(
        on_device,
        mesh=fine,
        in_specs=placed,
        out_specs=(P(None, None, TILE, None), P(None, None, TILE, None)),
        check_vma=False,
    )
```

time: 156 us -> 89.1 us (0.57)
  the two profiles are of different devices: /device:TPU:7 before, /device:TPU:1 now
where the time goes in v1:
time: 89.1 us; the launch traced here: 87.7 us
  starting transfers between devices  26.1 us (29%)
  waiting for transfers between devices  25.5 us (29%)
  blocking collectives  16.3 us (18%)
  other arithmetic  7.96 us (9%)
  Pallas kernels  5.88 us (7%)
  local copies, waits for them, and re-layouts  5.2 us (6%)
    all_to_all x2, waiting for transfers between devices, exchange(): return lax.all_to_all(value, axes, split_axis=0, concat_axis=0, tiled=True)  19.9 us
    all_to_all x1, blocking collectives, exchange(): return lax.all_to_all(value, axes, split_axis=0, concat_axis=0, tiled=True)  16.3 us
    all_to_all x2, starting transfers between devices, exchange(): return lax.all_to_all(value, axes, split_axis=0, concat_axis=0, tiled=True)  15.3 us
    ppermute x4, starting transfers between devices, swap_cores(): return lax.ppermute(value, 'c', [(0, 1), (1, 0)])  8.34 us
    pallas_call x1, Pallas kernels, angles(): pl.pallas_call(angles_kernel, out_shape=jax.ShapeDtypeStruct((2, depth, x...  5.88 us
    ppermute x4, waiting for transfers between devices, swap_cores(): return lax.ppermute(value, 'c', [(0, 1), (1, 0)])  2.8 us
    ppermute x1, waiting for transfers between devices, on_device(): far = lax.ppermute(jnp.where(core == 0, head, last), TILE, borders)  2.78 us
    ppermute x1, starting transfers between devices, on_device(): far = lax.ppermute(jnp.where(core == 0, head, last), TILE, borders)  2.43 us
  transfers between devices with their start and end apart: 7, of which 5 were waited for; matrix products, arithmetic and copies ran while one was open for 5% of the time, Pallas kernels for 0%

profile of v1, /device:TPU:1, one launch (start us, length us, event | category | flops | bytes accessed | tf_op | source)
XLA Modules:
  0.0 87.7 jit_solution(124418042579470734)
XLA Ops:
  0.6 0.9 %fusion.16 = (bf16[1,4,8,256]{3,2,1,0:T(8,128)(2,1)S(1)}, bf16[1,4,8,256]{3,2,1,0:T(8,128)(2,1)S(1)}) fusion(f32[4,8,256]{2,1,0:T(8,128)} %param.6, f32[4,8,256]{2,1,0:T(8,128)} %param.7), kind=kLoop, calls=%fused_computation.66 | loop fusion | flops 40960 | bytes 98304 | tf_op jit(solution)/shard_map/stack | solution.py:196
  1.6 0.9 broadcast_in_dim.13
  2.4 9.0 %all-to-all-start = ((bf16[16,2,4,8,256]{4,3,2,1,0:T(8,128)(2,1)}), bf16[16,2,4,8,256]{4,3,2,1,0:T(8,128)(2,1)S(1)}, u32[]{:S(2)}, u32[]{:S(2)}) async-start(bf16[16,2,4,8,256]{4,3,2,1,0:T(8,128)(2,1)} %broadcast_in_dim.13), calls=%async_computation | async-start | bytes 1048576 | tf_op jit(solution)/shard_map/all_to_all | solution.py:31
  12.2 0.7 copy-done.7
  12.9 12.3 %all-to-all-done.own = bf16[16,2,4,8,256]{4,3,2,1,0:T(8,128)(2,1)S(1)} async-done(((bf16[16,2,4,8,256]{4,3,2,1,0:T(8,128)(2,1)}), bf16[16,2,4,8,256]{4,3,2,1,0:T(8,128)(2,1)S(1)}, u32[]{:S(2)}, u32[]{:S(2)}) %all-to-all-start) | async-done | bytes 524320 | tf_op jit(solution)/shard_map/all_to_all | solution.py:31
  25.2 2.6 %collective-permute-start = (bf16[16,2,4,8,256]{4,3,2,1,0:T(8,128)(2,1)S(1)}, bf16[16,2,4,8,256]{4,3,2,1,0:T(8,128)(2,1)S(1)}, u32[]{:S(2)}, u32[]{:S(2)}) collective-permute-start(bf16[16,2,4,8,256]{4,3,2,1,0:T(8,128)(2,1)S(1)} %all-to-all-done.own), channel_id=1, source_target_pairs={{0,1},{1,0},{2,3},{3,2},{4,5},{5,4},{6,7},{7,6},{8,9},{9,8},{10,11... | collective-permute-start | bytes 1572872 | tf_op jit(solution)/shard_map/ppermute | solution.py:27
  28.6 1.0 %fusion.15 = bf16[256,256]{1,0:T(8,128)(2,1)S(1)} fusion(), kind=kLoop, calls=%fused_computation.56 | loop fusion | flops 1376256 | bytes 131072 | tf_op jit(solution)/shard_map/neg | solution.py:43
  29.6 1.1 %multiply_convert_fusion = (bf16[256,256]{1,0:T(8,128)(2,1)S(1)}, bf16[256,256]{1,0:T(8,128)(2,1)S(1)}) fusion(), kind=kLoop, calls=%fused_computation.18 | loop fusion | flops 1310720 | bytes 262144 | tf_op jit(solution)/shard_map/convert_element_type | solution.py:41
  30.8 1.1 %fusion.2 = (bf16[512,512]{1,0:T(8,128)(2,1)}, bf16[512,512]{1,0:T(8,128)(2,1)}) fusion(bf16[256,256]{1,0:T(8,128)(2,1)S(1)} %get-tuple-element.22, bf16[256,256]{1,0:T(8,128)(2,1)S(1)} %fusion.15, bf16[256,256]{1,0:T(8,128)(2,1)S(1)} %get-tuple-element.21), kind=kLoop, calls=%fused_computation.7 | loop fusion | flops 3670016 | bytes 1441792 | tf_op jit(solution)/shard_map/concatenate | solution.py:45
  31.8 0.8 copy-done.2
  32.6 5.9 %angles.1 = bf16[2,4,4,4,16,256]{5,4,3,2,1,0:T(8,128)(2,1)} custom-call(s32[9]{0:T(128)} %pad_add_fusion.1.numbers, bf16[16,2,4,8,256]{4,3,2,1,0:T(8,128)(2,1)} %copy-done.1, bf16[16,2,4,8,256]{4,3,2,1,0:T(8,128)(2,1)} %copy-done.2, bf16[512,512]{1,0:T(8,128)(2,1)} %get-tuple-element.11.forward, bf16[512,512]{1,0:T(8,128)(2,1)} %get-tuple-element.10.backward, ...), custom_call_target="tpu_custom_call" | custom-call | tf_op jit(solution)/shard_map/angles/pallas_call | solution.py:145
  38.5 1.2 %slice_bitcast_fusion = bf16[4,4,4,16,256]{4,3,2,1,0:T(8,128)(2,1)S(1)} fusion(bf16[2,4,4,4,16,256]{5,4,3,2,1,0:T(8,128)(2,1)} %angles.1), kind=kLoop, calls=%fused_computation.8 | loop fusion | bytes 1048576 | tf_op jit(solution)/shard_map/squeeze | solution.py:208
  39.8 1.9 %collective-permute-done.1 = bf16[4,4,4,16,256]{4,3,2,1,0:T(8,128)(2,1)S(1)} collective-permute-done((bf16[4,4,4,16,256]{4,3,2,1,0:T(8,128)(2,1)S(1)}, bf16[4,4,4,16,256]{4,3,2,1,0:T(8,128)(2,1)S(1)}, u32[]{:S(2)}, u32[]{:S(2)}) %collective-permute-start.1) | collective-permute-done | bytes 524320 | tf_op jit(solution)/shard_map/ppermute | solution.py:27
  41.9 16.3 %all_to_all.15 = bf16[16,4,16,256]{3,2,1,0:T(8,128)(2,1)S(1)} all-to-all(bf16[16,4,16,256]{3,2,1,0:T(8,128)(2,1)S(1)} %bitcast.33), channel_id=1, replica_groups=mesh['y'=4,'zh'=2,'zl'=4,'x'=4,'c'=2] {'y','x'}, dimensions={0} | all-to-all | bytes 1048576 | tf_op jit(solution)/shard_map/all_to_all | solution.py:31
  58.2 0.7 broadcast_in_dim.28
  59.0 6.3 %all-to-all-start.2 = ((bf16[32,16,256]{2,1,0:T(8,128)(2,1)}), bf16[32,16,256]{2,1,0:T(8,128)(2,1)S(1)}, u32[]{:S(2)}, u32[]{:S(2)}) async-start(bf16[32,16,256]{2,1,0:T(8,128)(2,1)} %bitcast.10), calls=%async_computation.2 | async-start | bytes 524288 | tf_op jit(solution)/shard_map/all_to_all | solution.py:31
  65.3 1.9 %collective-permute-start.4 = (f32[2,4,8,256]{3,2,1,0:T(8,128)S(1)}, f32[2,4,8,256]{3,2,1,0:T(8,128)S(1)}, u32[]{:S(2)}, u32[]{:S(2)}) collective-permute-start(f32[2,4,8,256]{3,2,1,0:T(8,128)S(1)} %pad_maximum_fusion.6), channel_id=1, source_target_pairs={{0,1},{1,0},{2,3},{3,2},{4,5},{5,4},{6,7},{7,6},{8,9},{9,8},{10,11... | collective-permute-start | bytes 196616 | tf_op jit(solution)/shard_map/ppermute | solution.py:27
  67.3 7.6 %all-to-all-done.2 = bf16[32,16,256]{2,1,0:T(8,128)(2,1)S(1)} async-done(((bf16[32,16,256]{2,1,0:T(8,128)(2,1)}), bf16[32,16,256]{2,1,0:T(8,128)(2,1)S(1)}, u32[]{:S(2)}, u32[]{:S(2)}) %all-to-all-start.2) | async-done | bytes 262176 | tf_op jit(solution)/shard_map/all_to_all | solution.py:31
  75.0 3.7 %collective-permute-start.2 = (f32[4,16,256]{2,1,0:T(8,128)S(1)}, f32[4,16,256]{2,1,0:T(8,128)S(1)}, u32[]{:S(2)}, u32[]{:S(2)}) collective-permute-start(f32[4,16,256]{2,1,0:T(8,128)S(1)} %broadcast_multiply_fusion), channel_id=1, source_target_pairs={{0,1},{1,0},{2,3},{3,2},{4,5},{5,4},{6,7},{7,6},{8,9},{9,8},{10,11... | collective-permute-start | bytes 196616 | tf_op jit(solution)/shard_map/ppermute | solution.py:27
  78.7 0.9 %collective-permute-done.2 = f32[4,16,256]{2,1,0:T(8,128)S(1)} collective-permute-done((f32[4,16,256]{2,1,0:T(8,128)S(1)}, f32[4,16,256]{2,1,0:T(8,128)S(1)}, u32[]{:S(2)}, u32[]{:S(2)}) %collective-permute-start.2) | collective-permute-done | bytes 65568 | tf_op jit(solution)/shard_map/ppermute | solution.py:27
  79.6 0.7 multiply_subtract_fusion.1
  80.3 2.4 %collective-permute-start.3 = (f32[2,4,3,256]{3,2,1,0:T(4,128)S(1)}, f32[2,4,3,256]{3,2,1,0:T(4,128)S(1)}, u32[]{:S(2)}, u32[]{:S(2)}) collective-permute-start(f32[2,4,3,256]{3,2,1,0:T(4,128)S(1)} %slice_select_fusion.2), channel_id=1, source_target_pairs={{1,2},{3,4},{5,6},{7,8},{9,10},{11,12},{13,14},{15,16},{17,18},{19... | collective-permute-start | bytes 73736 | tf_op jit(solution)/shard_map/ppermute | solution.py:231
  82.7 2.8 %collective-permute-done.3 = f32[2,4,3,256]{3,2,1,0:T(4,128)S(1)} collective-permute-done((f32[2,4,3,256]{3,2,1,0:T(4,128)S(1)}, f32[2,4,3,256]{3,2,1,0:T(4,128)S(1)}, u32[]{:S(2)}, u32[]{:S(2)}) %collective-permute-start.3) | collective-permute-done | bytes 24608 | tf_op jit(solution)/shard_map/ppermute | solution.py:231
  87.0 0.7 slice_add_fusion
  (49 shorter events, 3.5 us)
Async XLA Ops:
  2.4 22.8 %all-to-all-start = ((bf16[16,2,4,8,256]{4,3,2,1,0:T(8,128)(2,1)}), bf16[16,2,4,8,256]{4,3,2,1,0:T(8,128)(2,1)S(1)}, u32[]{:S(2)}, u32[]{:S(2)}) async-start(bf16[16,2,4,8,256]{4,3,2,1,0:T(8,128)(2,1)} %broadcast_in_dim.13), calls=%async_computation | async-start | bytes 1048576 | tf_op jit(solution)/shard_map/all_to_all | solution.py:31
  11.4 0.7 copy-start.6
  12.2 0.7 copy-start.7
  12.8 15.0 %copy-start.5 = (s32[2,2]{1,0:T(2,128)S(1)}, s32[2,2]{1,0:T(2,128)}, u32[]{:S(2)}) copy-start(s32[2,2]{1,0:T(2,128)} %param.8) | copy-start | bytes 52
  25.2 6.6 %copy-start.1 = (bf16[16,2,4,8,256]{4,3,2,1,0:T(8,128)(2,1)}, bf16[16,2,4,8,256]{4,3,2,1,0:T(8,128)(2,1)S(1)}, u32[]{:S(2)}) copy-start(bf16[16,2,4,8,256]{4,3,2,1,0:T(8,128)(2,1)S(1)} %all-to-all-done.own) | copy-start | bytes 1572868
  25.2 6.6 %collective-permute-start = (bf16[16,2,4,8,256]{4,3,2,1,0:T(8,128)(2,1)S(1)}, bf16[16,2,4,8,256]{4,3,2,1,0:T(8,128)(2,1)S(1)}, u32[]{:S(2)}, u32[]{:S(2)}) collective-permute-start(bf16[16,2,4,8,256]{4,3,2,1,0:T(8,128)(2,1)S(1)} %all-to-all-done.own), channel_id=1, source_target_pairs={{0,1},{1,0},{2,3},{3,2},{4,5},{5,4},{6,7},{7,6},{8,9},{9,8},{10,11... | collective-permute-start | bytes 1572872 | tf_op jit(solution)/shard_map/ppermute | solution.py:27
  31.8 0.8 copy-start.2
  38.5 3.2 %copy-start = (bf16[2,4,4,4,16,256]{5,4,3,2,1,0:T(8,128)(2,1)S(1)}, bf16[2,4,4,4,16,256]{5,4,3,2,1,0:T(8,128)(2,1)}, u32[]{:S(2)}) copy-start(bf16[2,4,4,4,16,256]{5,4,3,2,1,0:T(8,128)(2,1)} %angles.1) | copy-start | bytes 3145732
  39.7 2.0 %collective-permute-start.1 = (bf16[4,4,4,16,256]{4,3,2,1,0:T(8,128)(2,1)S(1)}, bf16[4,4,4,16,256]{4,3,2,1,0:T(8,128)(2,1)S(1)}, u32[]{:S(2)}, u32[]{:S(2)}) collective-permute-start(bf16[4,4,4,16,256]{4,3,2,1,0:T(8,128)(2,1)S(1)} %slice_bitcast_fusion), channel_id=1, source_target_pairs={{0,1},{1,0},{2,3},{3,2},{4,5},{5,4},{6,7},{7,6},{8,9},{9,8},{10,11... | collective-permute-start | bytes 1572872 | tf_op jit(solution)/shard_map/ppermute | solution.py:27
  59.0 6.3 %copy-start.3 = (f32[4,8,256]{2,1,0:T(8,128)S(1)}, f32[4,8,256]{2,1,0:T(8,128)}, u32[]{:S(2)}) copy-start(f32[4,8,256]{2,1,0:T(8,128)} %param.7) | copy-start | bytes 98308
  59.0 6.3 %copy-start.4 = (f32[4,8,256]{2,1,0:T(8,128)S(1)}, f32[4,8,256]{2,1,0:T(8,128)}, u32[]{:S(2)}) copy-start(f32[4,8,256]{2,1,0:T(8,128)} %param.6) | copy-start | bytes 98308
  59.0 16.0 %all-to-all-start.2 = ((bf16[32,16,256]{2,1,0:T(8,128)(2,1)}), bf16[32,16,256]{2,1,0:T(8,128)(2,1)S(1)}, u32[]{:S(2)}, u32[]{:S(2)}) async-start(bf16[32,16,256]{2,1,0:T(8,128)(2,1)} %bitcast.10), calls=%async_computation.2 | async-start | bytes 524288 | tf_op jit(solution)/shard_map/all_to_all | solution.py:31
  65.3 14.3 %collective-permute-start.4 = (f32[2,4,8,256]{3,2,1,0:T(8,128)S(1)}, f32[2,4,8,256]{3,2,1,0:T(8,128)S(1)}, u32[]{:S(2)}, u32[]{:S(2)}) collective-permute-start(f32[2,4,8,256]{3,2,1,0:T(8,128)S(1)} %pad_maximum_fusion.6), channel_id=1, source_target_pairs={{0,1},{1,0},{2,3},{3,2},{4,5},{5,4},{6,7},{7,6},{8,9},{9,8},{10,11... | collective-permute-start | bytes 196616 | tf_op jit(solution)/shard_map/ppermute | solution.py:27
  75.0 4.6 %collective-permute-start.2 = (f32[4,16,256]{2,1,0:T(8,128)S(1)}, f32[4,16,256]{2,1,0:T(8,128)S(1)}, u32[]{:S(2)}, u32[]{:S(2)}) collective-permute-start(f32[4,16,256]{2,1,0:T(8,128)S(1)} %broadcast_multiply_fusion), channel_id=1, source_target_pairs={{0,1},{1,0},{2,3},{3,2},{4,5},{5,4},{6,7},{7,6},{8,9},{9,8},{10,11... | collective-permute-start | bytes 196616 | tf_op jit(solution)/shard_map/ppermute | solution.py:27
  80.3 5.2 %collective-permute-start.3 = (f32[2,4,3,256]{3,2,1,0:T(4,128)S(1)}, f32[2,4,3,256]{3,2,1,0:T(4,128)S(1)}, u32[]{:S(2)}, u32[]{:S(2)}) collective-permute-start(f32[2,4,3,256]{3,2,1,0:T(4,128)S(1)} %slice_select_fusion.2), channel_id=1, source_target_pairs={{1,2},{3,4},{5,6},{7,8},{9,10},{11,12},{13,14},{15,16},{17,18},{19... | collective-permute-start | bytes 73736 | tf_op jit(solution)/shard_map/ppermute | solution.py:231

commit v2 on v1

--- a/solution.py
+++ b/solution.py
@@ -31,28 +31,78 @@
     return lax.all_to_all(value, axes, split_axis=0, concat_axis=0, tiled=True)
 
 
-def propagator(length):
-    indices = jnp.arange(length, dtype=jnp.int32)
-    gaps = indices[:, None] - indices[None, :]
-    turns = (gaps * gaps) % (2 * length)
+def outgoing_kernel(phase, absorb, out):
+    decay = jnp.exp(-absorb[...])
+    angle = phase[...]
+    real = (decay * jnp.cos(angle)).astype(jnp.bfloat16)
+    imag = (decay * jnp.sin(angle)).astype(jnp.bfloat16)
+    for chip in range(out.shape[0]):
+        out[chip, 0] = real
+        out[chip, 1] = imag
+
+
+def outgoing(phase, absorb, chips):
+    vmem = pl.BlockSpec(memory_space=pltpu.VMEM)
+    return pl.pallas_call(
+        outgoing_kernel,
+        out_shape=jax.ShapeDtypeStruct((chips, 2, *phase.shape), jnp.bfloat16),
+        in_specs=[vmem] * 2,
+        out_specs=vmem,
+        compiler_params=pltpu.CompilerParams(vmem_limit_bytes=4 << 20),
+        name="transmission",
+    )(phase, absorb)
+
+
+def setup_kernel(tilts, forward, backward, waves):
+    slots, _, length, _ = waves.shape
+    rows = lax.broadcasted_iota(jnp.int32, (length, length), 0)
+    columns = lax.broadcasted_iota(jnp.int32, (length, length), 1)
+    gaps = rows - columns
+    turns = (gaps * gaps) & (2 * length - 1)
     phases = turns.astype(jnp.float32) * (math.pi / length) - math.pi / 4
     scale = 1.0 / math.sqrt(length)
-    real_part = (jnp.cos(phases) * scale).astype(jnp.bfloat16)
-    imag_part = (jnp.sin(phases) * scale).astype(jnp.bfloat16)
-    forward_sweep = jnp.concatenate(
-        [jnp.concatenate([real_part, -imag_part], 1), jnp.concatenate([imag_part, real_part], 1)], 0
-    )
-    backward_sweep = jnp.concatenate(
-        [jnp.concatenate([real_part, imag_part], 1), jnp.concatenate([-imag_part, real_part], 1)], 0
-    )
-    return (forward_sweep, backward_sweep)
+    real = (jnp.cos(phases) * scale).astype(jnp.bfloat16)
+    imag = jnp.sin(phases) * scale
+    minus = (-imag).astype(jnp.bfloat16)
+    imag = imag.astype(jnp.bfloat16)
+    for matrix, upper, lower in ((forward, minus, imag), (backward, imag, minus)):
+        matrix[:length, :length] = real
+        matrix[:length, length:] = upper
+        matrix[length:, :length] = lower
+        matrix[length:, length:] = real
+
+    def factor(tilt, axis):
+        shape = (length, 1) if axis == 0 else (1, length)
+        index = lax.broadcasted_iota(jnp.int32, shape, axis)
+        turns = (tilt * index) & (length - 1)
+        phases = turns.astype(jnp.float32) * (2.0 * math.pi / length)
+        return jnp.cos(phases), jnp.sin(phases)
+
+    for slot in range(slots):
+        row_cos, row_sin = factor(tilts[slot, 0], 0)
+        col_cos, col_sin = factor(tilts[slot, 1], 1)
+        waves[slot, 0] = row_cos * col_cos - row_sin * col_sin
+        waves[slot, 1] = row_cos * col_sin + row_sin * col_cos
+
+
+def setup(tilts, length):
+    slots = tilts.shape[0]
+    vmem = pl.BlockSpec(memory_space=pltpu.VMEM)
+    sweep = jax.ShapeDtypeStruct((2 * length, 2 * length), jnp.bfloat16)
+    return pl.pallas_call(
+        setup_kernel,
+        out_shape=(sweep, sweep, jax.ShapeDtypeStruct((slots, 2, length, length), jnp.float32)),
+        in_specs=[pl.BlockSpec(memory_space=pltpu.SMEM)],
+        out_specs=(vmem,) * 3,
+        compiler_params=pltpu.CompilerParams(vmem_limit_bytes=12 << 20),
+        name="sweeps_and_waves",
+    )(tilts)
 
 
 def angles_kernel(
-    numbers, own, other, forward, backward, measured, out, first, wide, tall, acc
+    numbers, own, other, forward, backward, waves, measured, keep, send, first, wide, tall, terms
 ):
-    length = acc.shape[2]
-    slots = measured.shape[1]
+    slots, _, length, _ = waves.shape
     core = numbers[0]
     mine_first = core == 0
 
@@ -63,23 +113,13 @@
         lower = jnp.where(mine_first, theirs, mine)
         return jnp.stack([upper, lower], 1).reshape(length, length)
 
-    def factor(tilt, axis):
-        shape = (length, 1) if axis == 0 else (1, length)
-        index = lax.broadcasted_iota(jnp.int32, shape, axis)
-        turns = (tilt * index) & (length - 1)
-        phases = turns.astype(jnp.float32) * (2.0 * math.pi / length)
-        return jnp.cos(phases), jnp.sin(phases)
-
     def span(slot):
         return slice(slot * length, (slot + 1) * length)
 
-    acc[...] = jnp.zeros_like(acc)
-    for slot in range(slots):
-        level = numbers[3 + 4 * slot]
-        row_cos, row_sin = factor(numbers[1 + 4 * slot], 0)
-        col_cos, col_sin = factor(numbers[2 + 4 * slot], 1)
-        wave_real = row_cos * col_cos - row_sin * col_sin
-        wave_imag = row_cos * col_sin + row_sin * col_cos
+    for slot in range(slots):
+        level = numbers[1 + 2 * slot]
+        wave_real = waves[slot, 0]
+        wave_imag = waves[slot, 1]
         first_real = slice_plane(0, level)
         first_imag = slice_plane(1, level)
         enter_real = wave_real * first_real - wave_imag * first_imag
@@ -94,8 +134,8 @@
         wide[span(slot), length:] = middle[length:, span(slot)].astype(jnp.bfloat16)
     spread = jnp.dot(wide[...], backward[...], preferred_element_type=jnp.float32)
     for slot in range(slots):
-        level = numbers[3 + 4 * slot]
-        active = numbers[4 + 4 * slot].astype(jnp.float32)
+        level = numbers[1 + 2 * slot]
+        active = numbers[2 + 2 * slot].astype(jnp.float32)
         prop_real = spread[span(slot), :length]
         prop_imag = spread[span(slot), length:]
         second_real = slice_plane(0, level + 1)
@@ -104,57 +144,62 @@
         outgoing_imag = prop_real * second_imag + prop_imag * second_real
         residual_real = (outgoing_real - measured[0, slot].astype(jnp.float32)) * active
         residual_imag = (outgoing_imag - measured[1, slot].astype(jnp.float32)) * active
-        acc[0, level + 1] += outgoing_real * residual_imag - outgoing_imag * residual_real
-        acc[1, level + 1] -= outgoing_real * residual_real + outgoing_imag * residual_imag
+        terms[0, 3 * slot + 1] = outgoing_real * residual_imag - outgoing_imag * residual_real
+        terms[1, 3 * slot + 1] = -(outgoing_real * residual_real + outgoing_imag * residual_imag)
         adj_real = second_real * residual_real + second_imag * residual_imag
         adj_imag = second_real * residual_imag - second_imag * residual_real
         tall[:length, span(slot)] = adj_real.astype(jnp.bfloat16)
         tall[length:, span(slot)] = adj_imag.astype(jnp.bfloat16)
+        for component in range(2):
+            terms[component, 3 * slot + 2] = jnp.zeros((length, length), jnp.float32)
     half = jnp.dot(backward[...], tall[...], preferred_element_type=jnp.float32)
     for slot in range(slots):
         wide[span(slot), :length] = half[:length, span(slot)].astype(jnp.bfloat16)
         wide[span(slot), length:] = half[length:, span(slot)].astype(jnp.bfloat16)
     back = jnp.dot(wide[...], forward[...], preferred_element_type=jnp.float32)
     for slot in range(slots):
-        level = numbers[3 + 4 * slot]
         enter_real = first[0, slot]
         enter_imag = first[1, slot]
         back_real = back[span(slot), :length]
         back_imag = back[span(slot), length:]
-        acc[0, level] += enter_real * back_imag - enter_imag * back_real
-        acc[1, level] -= enter_real * back_real + enter_imag * back_imag
-    columns = out.shape[2]
-    blocks = out.shape[3]
-    rows = out.shape[4]
-    for component in range(2):
-        place = jnp.where(core == component, 0, 1)
-        for level in range(acc.shape[1]):
-            plane = acc[component, level].astype(jnp.bfloat16)
-            plane = plane.reshape(blocks, columns, rows, length)
+        terms[0, 3 * slot] = enter_real * back_imag - enter_imag * back_real
+        terms[1, 3 * slot] = -(enter_real * back_real + enter_imag * back_imag)
+    depth, columns, blocks, rows, _ = keep.shape
+    for out, component in ((keep, core), (send, 1 - core)):
+        for level in range(depth):
+            plane = None
+            for slot in range(slots):
+                step = level - numbers[1 + 2 * slot]
+                which = jnp.where(step == 0, 0, jnp.where(step == 1, 1, 2))
+                part = terms[component, 3 * slot + which]
+                plane = part if plane is None else plane + part
+            plane = plane.astype(jnp.bfloat16).reshape(blocks, columns, rows, length)
             for column in range(columns):
-                out[place, level, column] = plane[:, column]
-
-
-def angles(numbers, own, other, forward, backward, measured):
+                out[level, column] = plane[:, column]
+
+
+def angles(numbers, own, other, forward, backward, waves, measured):
     length = measured.shape[-1]
     depth = own.shape[2]
     slots = measured.shape[1]
     strips = own.shape[0]
     zl, x = SIZES[2], SIZES[3]
     vmem = pl.BlockSpec(memory_space=pltpu.VMEM)
+    half = jax.ShapeDtypeStruct((depth, x, zl, length // strips, length), jnp.bfloat16)
     return pl.pallas_call(
         angles_kernel,
-        out_shape=jax.ShapeDtypeStruct((2, depth, x, zl, length // strips, length), jnp.bfloat16),
-        in_specs=[pl.BlockSpec(memory_space=pltpu.SMEM)] + [vmem] * 5,
-        out_specs=vmem,
+        out_shape=(half, half),
+        in_specs=[pl.BlockSpec(memory_space=pltpu.SMEM)] + [vmem] * 6,
+        out_specs=(vmem, vmem),
         scratch_shapes=[
             pltpu.VMEM((2, slots, length, length), jnp.float32),
             pltpu.VMEM((slots * length, 2 * length), jnp.bfloat16),
             pltpu.VMEM((2 * length, slots * length), jnp.bfloat16),
-            pltpu.VMEM((2, depth, length, length), jnp.float32),
+            pltpu.VMEM((2, 3 * slots, length, length), jnp.float32),
         ],
+        compiler_params=pltpu.CompilerParams(vmem_limit_bytes=24 << 20),
         name="angles",
-    )(numbers, own, other, forward, backward, measured)
+    )(numbers, own, other, forward, backward, waves, measured)
 
 
 def divergence(dual_rows, dual_cols, above):
@@ -192,20 +237,20 @@
     chips = length // (2 * strip)
     core = lax.axis_index("c")
 
-    decay = jnp.exp(-absorb)
-    local_trans = jnp.stack([decay * jnp.cos(phase), decay * jnp.sin(phase)]).astype(jnp.bfloat16)
-    own = exchange(jnp.broadcast_to(local_trans[None], (chips, *local_trans.shape)), CHIPS)
-    other = swap_cores(own)
+    own = exchange(outgoing(phase, absorb, chips), CHIPS)
     params = jnp.stack([phase, absorb])
     partner_params = swap_cores(params)
-
-    forward_sweep, backward_sweep = propagator(length)
+    forward_sweep, backward_sweep, waves = setup(tilts, length)
     numbers = jnp.concatenate(
-        [core[None].astype(jnp.int32), jnp.concatenate([tilts, windows[:, None], live[:, None]], 1).reshape(-1)]
-    )
-    halves = angles(numbers, own, other, forward_sweep, backward_sweep, measured)
-
-    pair = halves[0].astype(jnp.float32) + swap_cores(halves[1]).astype(jnp.float32)
+        [core[None].astype(jnp.int32), jnp.stack([windows, live], 1).reshape(-1)]
+    )
+    own, numbers, forward_sweep, backward_sweep, waves, params, partner_params = lax.optimization_barrier(
+        (own, numbers, forward_sweep, backward_sweep, waves, params, partner_params)
+    )
+    other = swap_cores(own)
+    keep, send = angles(numbers, own, other, forward_sweep, backward_sweep, waves, measured)
+
+    pair = keep.astype(jnp.float32) + swap_cores(send).astype(jnp.float32)
     y, x = SIZES[0], SIZES[3]
     pair = pair.astype(jnp.bfloat16).reshape(y * x, -1, 2 * strip, length)
     plane = exchange(pair, ("y", "x")).astype(jnp.float32).sum(0).astype(jnp.bfloat16)

time: 89.1 us -> 82.1 us (0.921)
  other arithmetic: 7.96 us -> 3.25 us
  local copies, waits for them, and re-layouts: 5.2 us -> 3.73 us
    all_to_all x2, waiting for transfers between devices: 19.9 us -> 18 us  [exchange(): return lax.all_to_all(value, axes, split_axis=0, concat_axis=0, tiled=True)]
    concatenate x3 -> x1, other arithmetic: 1.72 us -> 0.08 us  [on_device(): jnp.concatenate([core[None].astype(jnp.int32), jnp.stack([windows, live],...]
    ppermute x4, waiting for transfers between devices: 2.8 us -> 3.97 us  [swap_cores(): return lax.ppermute(value, 'c', [(0, 1), (1, 0)])]
    squeeze x1 -> x0, local copies, waits for them, and re-layouts: 1.17 us -> none  [on_device(): halves[1]]
    convert_element_type x1 -> x0, other arithmetic: 1.14 us -> none  [propagator(): imag_part = (jnp.sin(phases) * scale).astype(jnp.bfloat16)]
    broadcast_in_dim x3 -> x0, local copies, waits for them, and re-layouts: 1.05 us -> none  [the longest x1 0.87 us: on_device(): jnp.broadcast_to(local_trans[None], (chips, *local_trans.shape))]
    neg x1 -> x0, other arithmetic: 1.03 us -> none  [propagator(): -imag_part]
    another operation x2 -> x1, other arithmetic: 0.91 us -> 0.01 us  [on_device(): jnp.stack([windows, live], 1).reshape(-1)]
  transfers between devices with their start and end apart: 7 -> 7, of which waited for: 5 -> 6; matrix products, arithmetic and copies ran while one was open for 5% -> 0% of each run, Pallas kernels for 0% -> 3%
where the time goes in v2:
time: 82.1 us; the launch traced here: 80.8 us
  starting transfers between devices  25.6 us (31%)
  waiting for transfers between devices  25 us (30%)
  blocking collectives  16.1 us (20%)
  Pallas kernels  6.31 us (8%)
  local copies, waits for them, and re-layouts  3.73 us (5%)
  other arithmetic  3.25 us (4%)
  between operations  0.84 us (1%)
    all_to_all x2, waiting for transfers between devices, exchange(): return lax.all_to_all(value, axes, split_axis=0, concat_axis=0, tiled=True)  18 us
    all_to_all x1, blocking collectives, exchange(): return lax.all_to_all(value, axes, split_axis=0, concat_axis=0, tiled=True)  16.1 us
    all_to_all x2, starting transfers between devices, exchange(): return lax.all_to_all(value, axes, split_axis=0, concat_axis=0, tiled=True)  15.6 us
    ppermute x4, starting transfers between devices, swap_cores(): return lax.ppermute(value, 'c', [(0, 1), (1, 0)])  7.85 us
    ppermute x4, waiting for transfers between devices, swap_cores(): return lax.ppermute(value, 'c', [(0, 1), (1, 0)])  3.97 us
    ppermute x1, waiting for transfers between devices, on_device(): far = lax.ppermute(jnp.where(core == 0, head, last), TILE, borders)  3.03 us
    unnamed x16, local copies, waits for them, and re-layouts  2.79 us
    pallas_call x1, Pallas kernels, setup(): pl.pallas_call(setup_kernel, out_shape=(sweep, sweep, jax.ShapeDtypeStruc...  2.72 us
  transfers between devices with their start and end apart: 7, of which 6 were waited for; matrix products, arithmetic and copies ran while one was open for 0% of the time, Pallas kernels for 3%

profile of v2, /device:TPU:1, one launch (start us, length us, event | category | flops | bytes accessed | tf_op | source)
XLA Modules:
  0.0 80.8 jit_solution(6691349668516129530)
XLA Ops:
  0.6 0.7 copy-done.1
  1.4 0.8 copy-done.3
  2.1 0.9 %transmission.1 = bf16[16,2,4,8,256]{4,3,2,1,0:T(8,128)(2,1)} custom-call(f32[4,8,256]{2,1,0:T(8,128)S(1)} %copy-done.3, f32[4,8,256]{2,1,0:T(8,128)S(1)} %copy-done.1), custom_call_target="tpu_custom_call" | custom-call | tf_op jit(solution)/shard_map/transmission/pallas_call | solution.py:46
  3.1 9.1 %all-to-all-start = ((bf16[16,2,4,8,256]{4,3,2,1,0:T(8,128)(2,1)}), bf16[16,2,4,8,256]{4,3,2,1,0:T(8,128)(2,1)S(1)}, u32[]{:S(2)}, u32[]{:S(2)}) async-start(bf16[16,2,4,8,256]{4,3,2,1,0:T(8,128)(2,1)} %transmission.1), calls=%async_computation | async-start | bytes 1048576 | tf_op jit(solution)/shard_map/all_to_all | solution.py:31
  12.3 1.0 %collective-permute-start = (f32[2,4,8,256]{3,2,1,0:T(8,128)S(1)}, f32[2,4,8,256]{3,2,1,0:T(8,128)S(1)}, u32[]{:S(2)}, u32[]{:S(2)}) collective-permute-start(f32[2,4,8,256]{3,2,1,0:T(8,128)S(1)} %pad_maximum_fusion.2), channel_id=1, source_target_pairs={{0,1},{1,0},{2,3},{3,2},{4,5},{5,4},{6,7},{7,6},{8,9},{9,8},{10,11... | collective-permute-start | bytes 196616 | tf_op jit(solution)/shard_map/ppermute | solution.py:27
  13.3 0.7 copy-done.6
  14.2 0.6 copy-done.5
  14.8 2.7 %sweeps_and_waves.1 = (bf16[512,512]{1,0:T(8,128)(2,1)S(1)}, bf16[512,512]{1,0:T(8,128)(2,1)S(1)}, f32[2,2,256,256]{3,2,1,0:T(8,128)S(1)}) custom-call(s32[2,2]{1,0:T(2,128)S(1)} %copy-done.5), custom_call_target="tpu_custom_call" | custom-call | tf_op jit(solution)/shard_map/sweeps_and_waves/pallas_call | solution.py:92
  17.6 8.4 %all-to-all-done.own = bf16[16,2,4,8,256]{4,3,2,1,0:T(8,128)(2,1)S(1)} async-done(((bf16[16,2,4,8,256]{4,3,2,1,0:T(8,128)(2,1)}), bf16[16,2,4,8,256]{4,3,2,1,0:T(8,128)(2,1)S(1)}, u32[]{:S(2)}, u32[]{:S(2)}) %all-to-all-start) | async-done | bytes 524320 | tf_op jit(solution)/shard_map/all_to_all | solution.py:31
  26.0 2.6 %collective-permute-start.1 = (bf16[16,2,4,8,256]{4,3,2,1,0:T(8,128)(2,1)S(1)}, bf16[16,2,4,8,256]{4,3,2,1,0:T(8,128)(2,1)S(1)}, u32[]{:S(2)}, u32[]{:S(2)}) collective-permute-start(bf16[16,2,4,8,256]{4,3,2,1,0:T(8,128)(2,1)S(1)} %all-to-all-done.own), channel_id=1, source_target_pairs={{0,1},{1,0},{2,3},{3,2},{4,5},{5,4},{6,7},{7,6},{8,9},{9,8},{10,11... | collective-permute-start | bytes 1572872 | tf_op jit(solution)/shard_map/ppermute | solution.py:27
  28.7 1.5 %collective-permute-done.1.other = bf16[16,2,4,8,256]{4,3,2,1,0:T(8,128)(2,1)S(1)} collective-permute-done((bf16[16,2,4,8,256]{4,3,2,1,0:T(8,128)(2,1)S(1)}, bf16[16,2,4,8,256]{4,3,2,1,0:T(8,128)(2,1)S(1)}, u32[]{:S(2)}, u32[]{:S(2)}) %collective-permute-start.1) | collective-permute-done | bytes 524320 | tf_op jit(solution)/shard_map/ppermute | solution.py:27
  30.2 2.6 %angles.1 = (bf16[4,4,4,16,256]{4,3,2,1,0:T(8,128)(2,1)S(1)}, bf16[4,4,4,16,256]{4,3,2,1,0:T(8,128)(2,1)S(1)}) custom-call(s32[5]{0:T(128)S(1)} %pad_add_fusion.1.numbers, bf16[16,2,4,8,256]{4,3,2,1,0:T(8,128)(2,1)S(1)} %all-to-all-done.own, bf16[16,2,4,8,256]{4,3,2,1,0:T(8,128)(2,1)S(1)} %collective-permute-done.1.other, ...), custom_call_target="tpu_custom_call" | custom-call | tf_op jit(solution)/shard_map/angles/pallas_call | solution.py:189
  32.9 0.5 collective-permute-start.2
  33.3 1.5 %collective-permute-done.2 = bf16[4,4,4,16,256]{4,3,2,1,0:T(8,128)(2,1)S(1)} collective-permute-done((bf16[4,4,4,16,256]{4,3,2,1,0:T(8,128)(2,1)S(1)}, bf16[4,4,4,16,256]{4,3,2,1,0:T(8,128)(2,1)S(1)}, u32[]{:S(2)}, u32[]{:S(2)}) %collective-permute-start.2) | collective-permute-done | bytes 524320 | tf_op jit(solution)/shard_map/ppermute | solution.py:27
  35.0 16.1 %all_to_all.15 = bf16[16,4,16,256]{3,2,1,0:T(8,128)(2,1)S(1)} all-to-all(bf16[16,4,16,256]{3,2,1,0:T(8,128)(2,1)S(1)} %bitcast.24), channel_id=1, replica_groups=mesh['y'=4,'zh'=2,'zl'=4,'x'=4,'c'=2] {'y','x'}, dimensions={0} | all-to-all | bytes 1048576 | tf_op jit(solution)/shard_map/all_to_all | solution.py:31
  51.2 0.7 broadcast_in_dim.5
  51.9 6.4 %all-to-all-start.2 = ((bf16[32,16,256]{2,1,0:T(8,128)(2,1)}), bf16[32,16,256]{2,1,0:T(8,128)(2,1)S(1)}, u32[]{:S(2)}, u32[]{:S(2)}) async-start(bf16[32,16,256]{2,1,0:T(8,128)(2,1)} %bitcast.6), calls=%async_computation.2 | async-start | bytes 524288 | tf_op jit(solution)/shard_map/all_to_all | solution.py:31
  58.5 9.6 %all-to-all-done.2 = bf16[32,16,256]{2,1,0:T(8,128)(2,1)S(1)} async-done(((bf16[32,16,256]{2,1,0:T(8,128)(2,1)}), bf16[32,16,256]{2,1,0:T(8,128)(2,1)S(1)}, u32[]{:S(2)}, u32[]{:S(2)}) %all-to-all-start.2) | async-done | bytes 262176 | tf_op jit(solution)/shard_map/all_to_all | solution.py:31
  68.1 3.7 %collective-permute-start.3 = (f32[4,16,256]{2,1,0:T(8,128)S(1)}, f32[4,16,256]{2,1,0:T(8,128)S(1)}, u32[]{:S(2)}, u32[]{:S(2)}) collective-permute-start(f32[4,16,256]{2,1,0:T(8,128)S(1)} %broadcast_multiply_fusion), channel_id=1, source_target_pairs={{0,1},{1,0},{2,3},{3,2},{4,5},{5,4},{6,7},{7,6},{8,9},{9,8},{10,11... | collective-permute-start | bytes 196616 | tf_op jit(solution)/shard_map/ppermute | solution.py:27
  71.8 0.9 %collective-permute-done.3 = f32[4,16,256]{2,1,0:T(8,128)S(1)} collective-permute-done((f32[4,16,256]{2,1,0:T(8,128)S(1)}, f32[4,16,256]{2,1,0:T(8,128)S(1)}, u32[]{:S(2)}, u32[]{:S(2)}) %collective-permute-start.3) | collective-permute-done | bytes 65568 | tf_op jit(solution)/shard_map/ppermute | solution.py:27
  72.7 0.6 multiply_subtract_fusion.1
  73.4 2.2 %collective-permute-start.4 = (f32[2,4,3,256]{3,2,1,0:T(4,128)S(1)}, f32[2,4,3,256]{3,2,1,0:T(4,128)S(1)}, u32[]{:S(2)}, u32[]{:S(2)}) collective-permute-start(f32[2,4,3,256]{3,2,1,0:T(4,128)S(1)} %slice_select_fusion.2), channel_id=1, source_target_pairs={{1,2},{3,4},{5,6},{7,8},{9,10},{11,12},{13,14},{15,16},{17,18},{19... | collective-permute-start | bytes 73736 | tf_op jit(solution)/shard_map/ppermute | solution.py:276
  75.6 3.0 %collective-permute-done.4 = f32[2,4,3,256]{3,2,1,0:T(4,128)S(1)} collective-permute-done((f32[2,4,3,256]{3,2,1,0:T(4,128)S(1)}, f32[2,4,3,256]{3,2,1,0:T(4,128)S(1)}, u32[]{:S(2)}, u32[]{:S(2)}) %collective-permute-start.4) | collective-permute-done | bytes 24608 | tf_op jit(solution)/shard_map/ppermute | solution.py:276
  80.1 0.7 slice_add_fusion
  (43 shorter events, 2.1 us)
Async XLA Ops:
  0.6 0.8 copy-start.1
  1.4 0.8 copy-start.3
  3.1 9.2 %copy-start.2 = (f32[4,8,256]{2,1,0:T(8,128)S(1)}, f32[4,8,256]{2,1,0:T(8,128)}, u32[]{:S(2)}) copy-start(f32[4,8,256]{2,1,0:T(8,128)} %absorb.1) | copy-start | bytes 98308
  3.1 9.2 %copy-start.4 = (f32[4,8,256]{2,1,0:T(8,128)S(1)}, f32[4,8,256]{2,1,0:T(8,128)}, u32[]{:S(2)}) copy-start(f32[4,8,256]{2,1,0:T(8,128)} %phase.1) | copy-start | bytes 98308
  3.1 27.1 %copy-start = (bf16[2,2,256,256]{3,2,1,0:T(8,128)(2,1)S(1)}, bf16[2,2,256,256]{3,2,1,0:T(8,128)(2,1)}, u32[]{:S(2)}) copy-start(bf16[2,2,256,256]{3,2,1,0:T(8,128)(2,1)} %measured.1) | copy-start | bytes 1572868
  3.1 22.9 %all-to-all-start = ((bf16[16,2,4,8,256]{4,3,2,1,0:T(8,128)(2,1)}), bf16[16,2,4,8,256]{4,3,2,1,0:T(8,128)(2,1)S(1)}, u32[]{:S(2)}, u32[]{:S(2)}) async-start(bf16[16,2,4,8,256]{4,3,2,1,0:T(8,128)(2,1)} %transmission.1), calls=%async_computation | async-start | bytes 1048576 | tf_op jit(solution)/shard_map/all_to_all | solution.py:31
  12.3 5.3 %collective-permute-start = (f32[2,4,8,256]{3,2,1,0:T(8,128)S(1)}, f32[2,4,8,256]{3,2,1,0:T(8,128)S(1)}, u32[]{:S(2)}, u32[]{:S(2)}) collective-permute-start(f32[2,4,8,256]{3,2,1,0:T(8,128)S(1)} %pad_maximum_fusion.2), channel_id=1, source_target_pairs={{0,1},{1,0},{2,3},{3,2},{4,5},{5,4},{6,7},{7,6},{8,9},{9,8},{10,11... | collective-permute-start | bytes 196616 | tf_op jit(solution)/shard_map/ppermute | solution.py:27
  13.3 0.7 copy-start.6
  13.3 0.7 copy-start.7
  14.1 0.7 copy-start.5
  26.0 4.2 %collective-permute-start.1 = (bf16[16,2,4,8,256]{4,3,2,1,0:T(8,128)(2,1)S(1)}, bf16[16,2,4,8,256]{4,3,2,1,0:T(8,128)(2,1)S(1)}, u32[]{:S(2)}, u32[]{:S(2)}) collective-permute-start(bf16[16,2,4,8,256]{4,3,2,1,0:T(8,128)(2,1)S(1)} %all-to-all-done.own), channel_id=1, source_target_pairs={{0,1},{1,0},{2,3},{3,2},{4,5},{5,4},{6,7},{7,6},{8,9},{9,8},{10,11... | collective-permute-start | bytes 1572872 | tf_op jit(solution)/shard_map/ppermute | solution.py:27
  32.9 2.0 %collective-permute-start.2 = (bf16[4,4,4,16,256]{4,3,2,1,0:T(8,128)(2,1)S(1)}, bf16[4,4,4,16,256]{4,3,2,1,0:T(8,128)(2,1)S(1)}, u32[]{:S(2)}, u32[]{:S(2)}) collective-permute-start(bf16[4,4,4,16,256]{4,3,2,1,0:T(8,128)(2,1)S(1)} %get-tuple-element.24), channel_id=1, source_target_pairs={{0,1},{1,0},{2,3},{3,2},{4,5},{5,4},{6,7},{7,6},{8,9},{9,8},{10,11... | collective-permute-start | bytes 1572872 | tf_op jit(solution)/shard_map/ppermute | solution.py:27
  51.9 16.1 %all-to-all-start.2 = ((bf16[32,16,256]{2,1,0:T(8,128)(2,1)}), bf16[32,16,256]{2,1,0:T(8,128)(2,1)S(1)}, u32[]{:S(2)}, u32[]{:S(2)}) async-start(bf16[32,16,256]{2,1,0:T(8,128)(2,1)} %bitcast.6), calls=%async_computation.2 | async-start | bytes 524288 | tf_op jit(solution)/shard_map/all_to_all | solution.py:31
  68.1 4.6 %collective-permute-start.3 = (f32[4,16,256]{2,1,0:T(8,128)S(1)}, f32[4,16,256]{2,1,0:T(8,128)S(1)}, u32[]{:S(2)}, u32[]{:S(2)}) collective-permute-start(f32[4,16,256]{2,1,0:T(8,128)S(1)} %broadcast_multiply_fusion), channel_id=1, source_target_pairs={{0,1},{1,0},{2,3},{3,2},{4,5},{5,4},{6,7},{7,6},{8,9},{9,8},{10,11... | collective-permute-start | bytes 196616 | tf_op jit(solution)/shard_map/ppermute | solution.py:27
  73.4 5.2 %collective-permute-start.4 = (f32[2,4,3,256]{3,2,1,0:T(4,128)S(1)}, f32[2,4,3,256]{3,2,1,0:T(4,128)S(1)}, u32[]{:S(2)}, u32[]{:S(2)}) collective-permute-start(f32[2,4,3,256]{3,2,1,0:T(4,128)S(1)} %slice_select_fusion.2), channel_id=1, source_target_pairs={{1,2},{3,4},{5,6},{7,8},{9,10},{11,12},{13,14},{15,16},{17,18},{19... | collective-permute-start | bytes 73736 | tf_op jit(solution)/shard_map/ppermute | solution.py:276

commit v3 on v2

--- a/solution.py
+++ b/solution.py
@@ -1,3 +1,4 @@
+import functools
 import math
 
 import jax
@@ -164,7 +165,9 @@
         back_imag = back[span(slot), length:]
         terms[0, 3 * slot] = enter_real * back_imag - enter_imag * back_real
         terms[1, 3 * slot] = -(enter_real * back_real + enter_imag * back_imag)
-    depth, columns, blocks, rows, _ = keep.shape
+    depth, columns, blocks, _, _ = keep.shape
+    strip = own.shape[3]
+    near = lax.broadcasted_iota(jnp.int32, (strip, length), 0) < strip // 2
     for out, component in ((keep, core), (send, 1 - core)):
         for level in range(depth):
             plane = None
@@ -173,19 +176,25 @@
                 which = jnp.where(step == 0, 0, jnp.where(step == 1, 1, 2))
                 part = terms[component, 3 * slot + which]
                 plane = part if plane is None else plane + part
-            plane = plane.astype(jnp.bfloat16).reshape(blocks, columns, rows, length)
             for column in range(columns):
-                out[level, column] = plane[:, column]
+                for block in range(blocks):
+                    start = (block * columns + column) * 2 * strip
+                    after = (start + 2 * strip) % length
+                    before = (start - strip) % length
+                    border = jnp.where(
+                        near, plane[after : after + strip], plane[before : before + strip]
+                    )
+                    rows = jnp.concatenate([plane[start : start + 2 * strip], border], 0)
+                    out[level, column, block] = rows.astype(jnp.bfloat16)
 
 
 def angles(numbers, own, other, forward, backward, waves, measured):
     length = measured.shape[-1]
     depth = own.shape[2]
     slots = measured.shape[1]
-    strips = own.shape[0]
     zl, x = SIZES[2], SIZES[3]
     vmem = pl.BlockSpec(memory_space=pltpu.VMEM)
-    half = jax.ShapeDtypeStruct((depth, x, zl, length // strips, length), jnp.bfloat16)
+    half = jax.ShapeDtypeStruct((depth, x, zl, 3 * own.shape[3], length), jnp.bfloat16)
     return pl.pallas_call(
         angles_kernel,
         out_shape=(half, half),
@@ -202,33 +211,61 @@
     )(numbers, own, other, forward, backward, waves, measured)
 
 
-def divergence(dual_rows, dual_cols, above):
-    shifted = jnp.concatenate([above, dual_rows[:, :, :-1, :]], 2)
-    left = jnp.pad(dual_cols[..., :-1], ((0, 0), (0, 0), (0, 0), (1, 0)))
-    return dual_rows - shifted + dual_cols - left
-
-
-def slopes(primal, below, keep_rows, inside):
-    shifted = jnp.concatenate([primal[:, :, 1:, :], below], 2)
-    diff_rows = (shifted - primal) * keep_rows
-    diff_cols = (
-        jnp.pad(primal[..., 1:] - primal[..., :-1], ((0, 0), (0, 0), (0, 0), (0, 1))) * inside
-    )
-    return (diff_rows, diff_cols)
-
-
-def dual_update(dual_rows, dual_cols, diff_rows, diff_cols):
-    new_rows = (dual_rows + TAU_DUAL * diff_rows) / (1.0 + TAU_DUAL * EPS_HUBER)
-    new_cols = (dual_cols + TAU_DUAL * diff_cols) / (1.0 + TAU_DUAL * EPS_HUBER)
-    scale = jnp.maximum(1.0, jnp.sqrt(new_rows * new_rows + new_cols * new_cols))
-    return (new_rows / scale, new_cols / scale)
-
-
-def row_masks(first_global, count, length):
-    global_rows = first_global + jnp.arange(count, dtype=jnp.int32)
-    inside = ((global_rows >= 0) & (global_rows < length)).astype(jnp.float32)
-    keep_rows = inside * (global_rows < length - 1).astype(jnp.float32)
-    return (keep_rows[:, None], inside[:, None])
+def regularize_kernel(numbers, column, params, mine, other, *, norm):
+    depth, ring, length = params.shape
+    owners = column.shape[0] // depth
+    strip = mine.shape[2]
+    mine_first = numbers[0] == 0
+    index = lax.broadcasted_iota(jnp.int32, (ring, length), 0)
+    rows = numbers[numbers.shape[0] - 1] + jnp.where(index < ring - strip // 2, index, index - ring)
+    keep_rows = (rows >= 0) & (rows < length - 1)
+    columns = lax.broadcasted_iota(jnp.int32, (ring, length), 1)
+    keep_cols = columns < length - 1
+    inner = columns > 0
+
+    def widened(start, dual_rows, dual_cols):
+        above = pltpu.roll(dual_rows, 1, 0)
+        left = jnp.where(inner, pltpu.roll(dual_cols, 1, 1), 0.0)
+        return start + LAMBDA_TV * (dual_rows - above + dual_cols - left)
+
+    for level in range(depth):
+        gradient = column[level * owners].astype(jnp.float32)
+        for owner in range(1, owners):
+            gradient = gradient + column[level * owners + owner].astype(jnp.float32)
+        gradient = gradient * norm
+        start = params[level] - STEP_SIZE * gradient
+        primal = start
+        dual_rows = dual_cols = None
+        for repeat in range(TV_STEPS):
+            step_rows = jnp.where(keep_rows, pltpu.roll(primal, ring - 1, 0) - primal, 0.0) * TAU_DUAL
+            step_cols = jnp.where(keep_cols, pltpu.roll(primal, length - 1, 1) - primal, 0.0) * TAU_DUAL
+            if repeat > 0:
+                step_rows = dual_rows + step_rows
+                step_cols = dual_cols + step_cols
+            dual_rows = step_rows / (1.0 + TAU_DUAL * EPS_HUBER)
+            dual_cols = step_cols / (1.0 + TAU_DUAL * EPS_HUBER)
+            scale = jnp.sqrt(jnp.maximum(1.0, dual_rows * dual_rows + dual_cols * dual_cols))
+            dual_rows = dual_rows / scale
+            dual_cols = dual_cols / scale
+            primal = widened(start, dual_rows, dual_cols)
+        for result, value in enumerate((gradient, primal)):
+            upper, lower = value[:strip], value[strip : 2 * strip]
+            mine[result, level] = jnp.where(mine_first, upper, lower)
+            other[result, level] = jnp.where(mine_first, lower, upper)
+
+
+def regularize(numbers, column, params, norm):
+    depth, ring, length = params.shape
+    vmem = pl.BlockSpec(memory_space=pltpu.VMEM)
+    half = jax.ShapeDtypeStruct((2, depth, ring // 3, length), jnp.float32)
+    return pl.pallas_call(
+        functools.partial(regularize_kernel, norm=norm),
+        out_shape=(half, half),
+        in_specs=[pl.BlockSpec(memory_space=pltpu.SMEM), vmem, vmem],
+        out_specs=(vmem, vmem),
+        compiler_params=pltpu.CompilerParams(vmem_limit_bytes=8 << 20),
+        name="regularize",
+    )(numbers, column, params)
 
 
 def on_device(phase, absorb, tilts, windows, live, measured):
@@ -236,60 +273,48 @@
     depth, strip, length = phase.shape
     chips = length // (2 * strip)
     core = lax.axis_index("c")
+    mine_first = core == 0
 
     own = exchange(outgoing(phase, absorb, chips), CHIPS)
     params = jnp.stack([phase, absorb])
-    partner_params = swap_cores(params)
+    tiles = 2 * chips
+    borders = [(i, i + 1) for i in range(1, tiles - 1, 2)]
+    borders = borders + [(j, i) for i, j in borders]
+    near = jnp.stack([params, lax.ppermute(params, TILE, borders)])
+    here = jnp.where(mine_first, near[:, 0], near[:, 1])
+    there = swap_cores(jnp.where(mine_first, near[:, 1], near[:, 0]))
+    upper, before = jnp.where(mine_first, here, there)
+    lower, after = jnp.where(mine_first, there, here)
+    half_strip = jnp.arange(strip)[:, None] < strip // 2
+    ring = jnp.concatenate([upper, lower, jnp.where(half_strip, after, before)], 1)
     forward_sweep, backward_sweep, waves = setup(tilts, length)
+    first_row = lax.axis_index(CHIPS) * (2 * strip)
     numbers = jnp.concatenate(
-        [core[None].astype(jnp.int32), jnp.stack([windows, live], 1).reshape(-1)]
-    )
-    own, numbers, forward_sweep, backward_sweep, waves, params, partner_params = lax.optimization_barrier(
-        (own, numbers, forward_sweep, backward_sweep, waves, params, partner_params)
+        [
+            core[None].astype(jnp.int32),
+            jnp.stack([windows, live], 1).reshape(-1),
+            first_row[None].astype(jnp.int32),
+        ]
+    )
+    own, numbers, forward_sweep, backward_sweep, waves, ring = lax.optimization_barrier(
+        (own, numbers, forward_sweep, backward_sweep, waves, ring)
     )
     other = swap_cores(own)
     keep, send = angles(numbers, own, other, forward_sweep, backward_sweep, waves, measured)
 
     pair = keep.astype(jnp.float32) + swap_cores(send).astype(jnp.float32)
     y, x = SIZES[0], SIZES[3]
-    pair = pair.astype(jnp.bfloat16).reshape(y * x, -1, 2 * strip, length)
+    pair = pair.astype(jnp.bfloat16).reshape(y * x, -1, *keep.shape[-2:])
     plane = exchange(pair, ("y", "x")).astype(jnp.float32).sum(0).astype(jnp.bfloat16)
     copies = SIZES[0] * SIZES[1]
     sent = jnp.broadcast_to(plane[None], (copies, *plane.shape)).reshape(-1, *plane.shape[1:])
-    column = exchange(sent, ("y", "zh", "zl")).astype(jnp.float32)
-    column = column.reshape(depth, -1, 2 * strip, length).sum(1)
+    column = exchange(sent, ("y", "zh", "zl"))
     all_slots = slots * math.prod(SIZES)
-    mine = column * (1.0 / math.sqrt(all_slots))
-    theirs = swap_cores(mine)
-    both = jnp.stack([jnp.where(core == 0, mine, theirs), jnp.where(core == 0, theirs, mine)])
-    upper, lower = both[:, :, :strip], both[:, :, strip:]
-    gradient = jnp.where(core == 0, upper, lower)
-    partner_gradient = jnp.where(core == 0, lower, upper)
-    volume = params - STEP_SIZE * gradient
-    partner_volume = partner_params - STEP_SIZE * partner_gradient
-
-    last = volume[:, :, strip - TV_STEPS :]
-    head = volume[:, :, :TV_STEPS]
-    tiles = SIZES[2] * SIZES[3] * SIZES[4]
-    borders = [(i, i + 1) for i in range(1, tiles - 1, 2)]
-    borders = borders + [(j, i) for i, j in borders]
-    far = lax.ppermute(jnp.where(core == 0, head, last), TILE, borders)
-    before = jnp.where(core == 0, far, partner_volume[:, :, strip - TV_STEPS :])
-    after = jnp.where(core == 0, partner_volume[:, :, :TV_STEPS], far)
-    extended = jnp.concatenate([before, volume, after], 2)
-
-    first_row = lax.axis_index(TILE) * strip
-    count = strip + 2 * TV_STEPS
-    keep_rows, inside = row_masks(first_row - TV_STEPS, count, length)
-    zero_row = jnp.zeros((2, depth, 1, length), jnp.float32)
-    dual_rows = jnp.zeros_like(extended)
-    dual_cols = jnp.zeros_like(extended)
-    for repeat in range(TV_STEPS):
-        primal = extended + LAMBDA_TV * divergence(dual_rows, dual_cols, zero_row)
-        diff_rows, diff_cols = slopes(primal, zero_row, keep_rows, inside)
-        dual_rows, dual_cols = dual_update(dual_rows, dual_cols, diff_rows, diff_cols)
-    wide_out = extended + LAMBDA_TV * divergence(dual_rows, dual_cols, zero_row)
-    volume_out = wide_out[:, :, TV_STEPS : TV_STEPS + strip, :]
+    mine, theirs = regularize(numbers, column, ring, 1.0 / math.sqrt(all_slots))
+    theirs = swap_cores(theirs)
+    gradient, volume_out = jnp.stack(
+        [jnp.where(mine_first, mine, theirs), jnp.where(mine_first, theirs, mine)], 1
+    )
     return (volume_out, gradient)
 
 

time: 82.1 us -> 83.7 us (1.019)
  blocking collectives: 16.1 us -> 35.9 us
  waiting for transfers between devices: 25 us -> 16.5 us
  starting transfers between devices: 25.6 us -> 18.6 us
  local copies, waits for them, and re-layouts: 3.73 us -> 1.74 us
  Pallas kernels: 6.31 us -> 7.56 us
  other arithmetic: 3.25 us -> 2.03 us
    all_to_all x1 -> x2, blocking collectives: 16.1 us -> 35.9 us  [exchange(): return lax.all_to_all(value, axes, split_axis=0, concat_axis=0, tiled=True)]
    all_to_all x2 -> x1, starting transfers between devices: 15.6 us -> 8.02 us  [exchange(): return lax.all_to_all(value, axes, split_axis=0, concat_axis=0, tiled=True)]
    all_to_all x2 -> x1, waiting for transfers between devices: 18 us -> 11 us  [exchange(): return lax.all_to_all(value, axes, split_axis=0, concat_axis=0, tiled=True)]
    ppermute x1, waiting for transfers between devices: 3.03 us -> 0.01 us  [on_device(): near = jnp.stack([params, lax.ppermute(params, TILE, borders)])]
    ppermute x1, starting transfers between devices: 2.19 us -> 4.51 us  [on_device(): near = jnp.stack([params, lax.ppermute(params, TILE, borders)])]
    ppermute x4, starting transfers between devices: 7.85 us -> 6.09 us  [swap_cores(): return lax.ppermute(value, 'c', [(0, 1), (1, 0)])]
    ppermute x4, waiting for transfers between devices: 3.97 us -> 5.52 us  [swap_cores(): return lax.ppermute(value, 'c', [(0, 1), (1, 0)])]
    another operation x2 -> x3, other arithmetic: 0.02 us -> 1.47 us  [the longest x1 0.8 us: on_device(): near = jnp.stack([params, lax.ppermute(params, TILE, borders)])]
  transfers between devices with their start and end apart: 7 -> 6, of which waited for: 6 -> 5; matrix products, arithmetic and copies ran while one was open for 0% -> 0% of each run, Pallas kernels for 3% -> 4%
where the time goes in v3:
time: 83.7 us; the launch traced here: 83.2 us
  blocking collectives  35.9 us (43%)
  starting transfers between devices  18.6 us (22%)
  waiting for transfers between devices  16.5 us (20%)
  Pallas kernels  7.56 us (9%)
  other arithmetic  2.03 us (2%)
  local copies, waits for them, and re-layouts  1.74 us (2%)
    all_to_all x2, blocking collectives, exchange(): return lax.all_to_all(value, axes, split_axis=0, concat_axis=0, tiled=True)  35.9 us
    all_to_all x1, waiting for transfers between devices, exchange(): return lax.all_to_all(value, axes, split_axis=0, concat_axis=0, tiled=True)  11 us
    all_to_all x1, starting transfers between devices, exchange(): return lax.all_to_all(value, axes, split_axis=0, concat_axis=0, tiled=True)  8.02 us
    ppermute x4, starting transfers between devices, swap_cores(): return lax.ppermute(value, 'c', [(0, 1), (1, 0)])  6.09 us
    ppermute x4, waiting for transfers between devices, swap_cores(): return lax.ppermute(value, 'c', [(0, 1), (1, 0)])  5.52 us
    ppermute x1, starting transfers between devices, on_device(): near = jnp.stack([params, lax.ppermute(params, TILE, borders)])  4.51 us
    pallas_call x1, Pallas kernels, angles(): pl.pallas_call(angles_kernel, out_shape=(half, half), in_specs=[pl.BlockS...  2.72 us
    pallas_call x1, Pallas kernels, setup(): pl.pallas_call(setup_kernel, out_shape=(sweep, sweep, jax.ShapeDtypeStruc...  2.72 us
  transfers between devices with their start and end apart: 6, of which 5 were waited for; matrix products, arithmetic and copies ran while one was open for 0% of the time, Pallas kernels for 4%

profile of v3, /device:TPU:1, one launch (start us, length us, event | category | flops | bytes accessed | tf_op | source)
XLA Modules:
  0.0 83.2 jit_solution(9953004187769273030)
XLA Ops:
  0.7 0.8 fusion.5
  1.5 4.5 %collective-permute-start = (f32[2,4,8,256]{3,2,1,0:T(8,128)S(1)}, f32[2,4,8,256]{3,2,1,0:T(8,128)S(1)}, u32[]{:S(2)}, u32[]{:S(2)}) collective-permute-start(f32[2,4,8,256]{3,2,1,0:T(8,128)S(1)} %get-tuple-element.35), channel_id=1, source_target_pairs={{1,2},{3,4},{5,6},{7,8},{9,10},{11,12},{13,14},{15,16},{17,18},{19... | collective-permute-start | bytes 196616 | tf_op jit(solution)/shard_map/ppermute | solution.py:283
  6.0 0.7 copy-done.1
  6.7 0.8 copy-done.2
  7.5 1.0 %transmission.1 = bf16[16,2,4,8,256]{4,3,2,1,0:T(8,128)(2,1)} custom-call(f32[4,8,256]{2,1,0:T(8,128)S(1)} %copy-done.1, f32[4,8,256]{2,1,0:T(8,128)S(1)} %copy-done.2), custom_call_target="tpu_custom_call" | custom-call | tf_op jit(solution)/shard_map/transmission/pallas_call | solution.py:47
  8.5 8.0 %all-to-all-start = ((bf16[16,2,4,8,256]{4,3,2,1,0:T(8,128)(2,1)}), bf16[16,2,4,8,256]{4,3,2,1,0:T(8,128)(2,1)S(1)}, u32[]{:S(2)}, u32[]{:S(2)}) async-start(bf16[16,2,4,8,256]{4,3,2,1,0:T(8,128)(2,1)} %transmission.1), calls=%async_computation | async-start | bytes 1048576 | tf_op jit(solution)/shard_map/all_to_all | solution.py:32
  16.5 0.1 copy.8
  16.7 2.7 %sweeps_and_waves.1 = (bf16[512,512]{1,0:T(8,128)(2,1)S(1)}, bf16[512,512]{1,0:T(8,128)(2,1)S(1)}, f32[2,2,256,256]{3,2,1,0:T(8,128)S(1)}) custom-call(s32[2,2]{1,0:T(2,128)S(1)} %copy-done.3), custom_call_target="tpu_custom_call" | custom-call | tf_op jit(solution)/shard_map/sweeps_and_waves/pallas_call | solution.py:93
  19.5 0.1 collective-permute-start.1
  19.7 1.2 %collective-permute-done.1 = f32[2,4,8,256]{3,2,1,0:T(8,128)S(1)} collective-permute-done((f32[2,4,8,256]{3,2,1,0:T(8,128)S(1)}, f32[2,4,8,256]{3,2,1,0:T(8,128)S(1)}, u32[]{:S(2)}, u32[]{:S(2)}) %collective-permute-start.1) | collective-permute-done | bytes 65568 | tf_op jit(solution)/shard_map/ppermute | solution.py:28
  21.0 11.0 %all-to-all-done.own = bf16[16,2,4,8,256]{4,3,2,1,0:T(8,128)(2,1)S(1)} async-done(((bf16[16,2,4,8,256]{4,3,2,1,0:T(8,128)(2,1)}), bf16[16,2,4,8,256]{4,3,2,1,0:T(8,128)(2,1)S(1)}, u32[]{:S(2)}, u32[]{:S(2)}) %all-to-all-start) | async-done | bytes 524320 | tf_op jit(solution)/shard_map/all_to_all | solution.py:32
  32.0 0.5 collective-permute-start.2
  32.5 1.5 %collective-permute-done.2.other = bf16[16,2,4,8,256]{4,3,2,1,0:T(8,128)(2,1)S(1)} collective-permute-done((bf16[16,2,4,8,256]{4,3,2,1,0:T(8,128)(2,1)S(1)}, bf16[16,2,4,8,256]{4,3,2,1,0:T(8,128)(2,1)S(1)}, u32[]{:S(2)}, u32[]{:S(2)}) %collective-permute-start.2) | collective-permute-done | bytes 524320 | tf_op jit(solution)/shard_map/ppermute | solution.py:28
  34.0 2.7 %angles.1 = (bf16[4,4,4,24,256]{4,3,2,1,0:T(8,128)(2,1)S(1)}, bf16[4,4,4,24,256]{4,3,2,1,0:T(8,128)(2,1)S(1)}) custom-call(s32[6]{0:T(128)S(1)} %pad_add_fusion.1.numbers, bf16[16,2,4,8,256]{4,3,2,1,0:T(8,128)(2,1)S(1)} %all-to-all-done.own, bf16[16,2,4,8,256]{4,3,2,1,0:T(8,128)(2,1)S(1)} %collective-permute-done.2.other, ...), custom_call_target="tpu_custom_call" | custom-call | tf_op jit(solution)/shard_map/angles/pallas_call | solution.py:198
  36.7 0.5 collective-permute-start.3
  37.2 1.9 %collective-permute-done.3 = bf16[4,4,4,24,256]{4,3,2,1,0:T(8,128)(2,1)S(1)} collective-permute-done((bf16[4,4,4,24,256]{4,3,2,1,0:T(8,128)(2,1)S(1)}, bf16[4,4,4,24,256]{4,3,2,1,0:T(8,128)(2,1)S(1)}, u32[]{:S(2)}, u32[]{:S(2)}) %collective-permute-start.3) | collective-permute-done | bytes 786464 | tf_op jit(solution)/shard_map/ppermute | solution.py:28
  39.1 0.2 add_convert_fusion
  39.4 18.8 %all_to_all.15 = bf16[16,4,24,256]{3,2,1,0:T(8,128)(2,1)S(1)} all-to-all(bf16[16,4,24,256]{3,2,1,0:T(8,128)(2,1)S(1)} %bitcast.40), channel_id=1, replica_groups=mesh['y'=4,'zh'=2,'zl'=4,'x'=4,'c'=2] {'y','x'}, dimensions={0} | all-to-all | bytes 1572864 | tf_op jit(solution)/shard_map/all_to_all | solution.py:32
  58.2 0.1 reduce_sum.12
  58.4 17.1 %all_to_all.16.column = bf16[32,24,256]{2,1,0:T(8,128)(2,1)S(1)} all-to-all(bf16[32,24,256]{2,1,0:T(8,128)(2,1)S(1)} %bitcast.41), channel_id=1, replica_groups=mesh['y'=4,'zh'=2,'zl'=4,'x'=4,'c'=2] {'y','zh','zl'}, dimensions={0} | all-to-all | bytes 786432 | tf_op jit(solution)/shard_map/all_to_all | solution.py:32
  75.4 1.2 %regularize.1 = (f32[2,4,8,256]{3,2,1,0:T(8,128)S(1)}, f32[2,4,8,256]{3,2,1,0:T(8,128)S(1)}) custom-call(s32[6]{0:T(128)S(1)} %pad_add_fusion.1.numbers, bf16[32,24,256]{2,1,0:T(8,128)(2,1)S(1)} %all_to_all.16.column, f32[4,24,256]{2,1,0:T(8,128)S(1)} %pad_maximum_fusion.params), custom_call_target="tpu_custom_call" | custom-call | tf_op jit(solution)/shard_map/regularize/pallas_call | solution.py:261
  76.6 5.0 %collective-permute-start.4 = (f32[2,4,8,256]{3,2,1,0:T(8,128)S(1)}, f32[2,4,8,256]{3,2,1,0:T(8,128)S(1)}, u32[]{:S(2)}, u32[]{:S(2)}) collective-permute-start(f32[2,4,8,256]{3,2,1,0:T(8,128)S(1)} %get-tuple-element.27), channel_id=1, source_target_pairs={{0,1},{1,0},{2,3},{3,2},{4,5},{5,4},{6,7},{7,6},{8,9},{9,8},{10,11... | collective-permute-start | bytes 196616 | tf_op jit(solution)/shard_map/ppermute | solution.py:28
  81.6 0.9 %collective-permute-done.4 = f32[2,4,8,256]{3,2,1,0:T(8,128)S(1)} collective-permute-done((f32[2,4,8,256]{3,2,1,0:T(8,128)S(1)}, f32[2,4,8,256]{3,2,1,0:T(8,128)S(1)}, u32[]{:S(2)}, u32[]{:S(2)}) %collective-permute-start.4) | collective-permute-done | bytes 65568 | tf_op jit(solution)/shard_map/ppermute | solution.py:28
  82.6 0.7 fusion.3
  (22 shorter events, 0.4 us)
Async XLA Ops:
  0.6 15.9 %copy-start.4 = (s32[2]{0:T(128)S(1)}, s32[2]{0:T(128)}, u32[]{:S(2)}) copy-start(s32[2]{0:T(128)} %param.10) | copy-start | bytes 28
  0.6 15.9 %copy-start.5 = (s32[2]{0:T(128)S(1)}, s32[2]{0:T(128)}, u32[]{:S(2)}) copy-start(s32[2]{0:T(128)} %param.9) | copy-start | bytes 28
  0.7 16.1 %copy-start.3 = (s32[2,2]{1,0:T(2,128)S(1)}, s32[2,2]{1,0:T(2,128)}, u32[]{:S(2)}) copy-start(s32[2,2]{1,0:T(2,128)} %tilts.1) | copy-start | bytes 52
  1.5 18.0 %collective-permute-start = (f32[2,4,8,256]{3,2,1,0:T(8,128)S(1)}, f32[2,4,8,256]{3,2,1,0:T(8,128)S(1)}, u32[]{:S(2)}, u32[]{:S(2)}) collective-permute-start(f32[2,4,8,256]{3,2,1,0:T(8,128)S(1)} %get-tuple-element.35), channel_id=1, source_target_pairs={{1,2},{3,4},{5,6},{7,8},{9,10},{11,12},{13,14},{15,16},{17,18},{19... | collective-permute-start | bytes 196616 | tf_op jit(solution)/shard_map/ppermute | solution.py:283
  6.0 0.8 copy-start.1
  6.7 0.8 copy-start.2
  8.5 25.5 %copy-start = (bf16[2,2,256,256]{3,2,1,0:T(8,128)(2,1)S(1)}, bf16[2,2,256,256]{3,2,1,0:T(8,128)(2,1)}, u32[]{:S(2)}) copy-start(bf16[2,2,256,256]{3,2,1,0:T(8,128)(2,1)} %measured.1) | copy-start | bytes 1572868
  8.5 23.5 %all-to-all-start = ((bf16[16,2,4,8,256]{4,3,2,1,0:T(8,128)(2,1)}), bf16[16,2,4,8,256]{4,3,2,1,0:T(8,128)(2,1)S(1)}, u32[]{:S(2)}, u32[]{:S(2)}) async-start(bf16[16,2,4,8,256]{4,3,2,1,0:T(8,128)(2,1)} %transmission.1), calls=%async_computation | async-start | bytes 1048576 | tf_op jit(solution)/shard_map/all_to_all | solution.py:32
  19.5 1.3 %collective-permute-start.1 = (f32[2,4,8,256]{3,2,1,0:T(8,128)S(1)}, f32[2,4,8,256]{3,2,1,0:T(8,128)S(1)}, u32[]{:S(2)}, u32[]{:S(2)}) collective-permute-start(f32[2,4,8,256]{3,2,1,0:T(8,128)S(1)} %select_bitcast_fusion.2), channel_id=1, source_target_pairs={{0,1},{1,0},{2,3},{3,2},{4,5},{5,4},{6,7},{7,6},{8,9},{9,8},{10,11... | collective-permute-start | bytes 196616 | tf_op jit(solution)/shard_map/ppermute | solution.py:28
  32.0 2.0 %collective-permute-start.2 = (bf16[16,2,4,8,256]{4,3,2,1,0:T(8,128)(2,1)S(1)}, bf16[16,2,4,8,256]{4,3,2,1,0:T(8,128)(2,1)S(1)}, u32[]{:S(2)}, u32[]{:S(2)}) collective-permute-start(bf16[16,2,4,8,256]{4,3,2,1,0:T(8,128)(2,1)S(1)} %all-to-all-done.own), channel_id=1, source_target_pairs={{0,1},{1,0},{2,3},{3,2},{4,5},{5,4},{6,7},{7,6},{8,9},{9,8},{10,11... | collective-permute-start | bytes 1572872 | tf_op jit(solution)/shard_map/ppermute | solution.py:28
  36.7 2.4 %collective-permute-start.3 = (bf16[4,4,4,24,256]{4,3,2,1,0:T(8,128)(2,1)S(1)}, bf16[4,4,4,24,256]{4,3,2,1,0:T(8,128)(2,1)S(1)}, u32[]{:S(2)}, u32[]{:S(2)}) collective-permute-start(bf16[4,4,4,24,256]{4,3,2,1,0:T(8,128)(2,1)S(1)} %get-tuple-element.24), channel_id=1, source_target_pairs={{0,1},{1,0},{2,3},{3,2},{4,5},{5,4},{6,7},{7,6},{8,9},{9,8},{10,11... | collective-permute-start | bytes 2359304 | tf_op jit(solution)/shard_map/ppermute | solution.py:28
  76.6 5.9 %collective-permute-start.4 = (f32[2,4,8,256]{3,2,1,0:T(8,128)S(1)}, f32[2,4,8,256]{3,2,1,0:T(8,128)S(1)}, u32[]{:S(2)}, u32[]{:S(2)}) collective-permute-start(f32[2,4,8,256]{3,2,1,0:T(8,128)S(1)} %get-tuple-element.27), channel_id=1, source_target_pairs={{0,1},{1,0},{2,3},{3,2},{4,5},{5,4},{6,7},{7,6},{8,9},{9,8},{10,11... | collective-permute-start | bytes 196616 | tf_op jit(solution)/shard_map/ppermute | solution.py:28

commit v4 on v3

--- a/solution.py
+++ b/solution.py
@@ -275,7 +275,11 @@
     core = lax.axis_index("c")
     mine_first = core == 0
 
-    own = exchange(outgoing(phase, absorb, chips), CHIPS)
+    sent = outgoing(phase, absorb, chips)
+    sent, tilts = lax.optimization_barrier((sent, tilts))
+    own = exchange(sent, CHIPS)
+    forward_sweep, backward_sweep, waves = setup(tilts, length)
+    phase, absorb, waves = lax.optimization_barrier((phase, absorb, waves))
     params = jnp.stack([phase, absorb])
     tiles = 2 * chips
     borders = [(i, i + 1) for i in range(1, tiles - 1, 2)]
@@ -287,7 +291,6 @@
     lower, after = jnp.where(mine_first, there, here)
     half_strip = jnp.arange(strip)[:, None] < strip // 2
     ring = jnp.concatenate([upper, lower, jnp.where(half_strip, after, before)], 1)
-    forward_sweep, backward_sweep, waves = setup(tilts, length)
     first_row = lax.axis_index(CHIPS) * (2 * strip)
     numbers = jnp.concatenate(
         [

time: 83.7 us -> 80.6 us (0.963)
  waiting for transfers between devices: 16.5 us -> 10.4 us
  starting transfers between devices: 18.6 us -> 21.6 us
  blocking collectives: 35.9 us -> 36.8 us
    all_to_all x1, waiting for transfers between devices: 11 us -> 2.68 us  [exchange(): return lax.all_to_all(value, axes, split_axis=0, concat_axis=0, tiled=True)]
    ppermute x1, waiting for transfers between devices: 0.01 us -> 2.23 us  [on_device(): near = jnp.stack([params, lax.ppermute(params, TILE, borders)])]
    ppermute x4, starting transfers between devices: 6.09 us -> 8.06 us  [swap_cores(): return lax.ppermute(value, 'c', [(0, 1), (1, 0)])]
    all_to_all x1, starting transfers between devices: 8.02 us -> 9.15 us  [exchange(): return lax.all_to_all(value, axes, split_axis=0, concat_axis=0, tiled=True)]
    all_to_all x2, blocking collectives: 35.9 us -> 36.8 us  [exchange(): return lax.all_to_all(value, axes, split_axis=0, concat_axis=0, tiled=True)]
  transfers between devices with their start and end apart: 6 -> 6, of which waited for: 5 -> 6; matrix products, arithmetic and copies ran while one was open for 0% -> 0% of each run, Pallas kernels for 4% -> 3%
where the time goes in v4:
time: 80.6 us; the launch traced here: 80.2 us
  blocking collectives  36.8 us (46%)
  starting transfers between devices  21.6 us (27%)
  waiting for transfers between devices  10.4 us (13%)
  Pallas kernels  7.55 us (9%)
  local copies, waits for them, and re-layouts  1.74 us (2%)
  other arithmetic  1.24 us (2%)
    all_to_all x2, blocking collectives, exchange(): return lax.all_to_all(value, axes, split_axis=0, concat_axis=0, tiled=True)  36.8 us
    all_to_all x1, starting transfers between devices, exchange(): return lax.all_to_all(value, axes, split_axis=0, concat_axis=0, tiled=True)  9.15 us
    ppermute x4, starting transfers between devices, swap_cores(): return lax.ppermute(value, 'c', [(0, 1), (1, 0)])  8.06 us
    ppermute x4, waiting for transfers between devices, swap_cores(): return lax.ppermute(value, 'c', [(0, 1), (1, 0)])  5.52 us
    ppermute x1, starting transfers between devices, on_device(): near = jnp.stack([params, lax.ppermute(params, TILE, borders)])  4.39 us
    pallas_call x1, Pallas kernels, angles(): pl.pallas_call(angles_kernel, out_shape=(half, half), in_specs=[pl.BlockS...  2.72 us
    pallas_call x1, Pallas kernels, setup(): pl.pallas_call(setup_kernel, out_shape=(sweep, sweep, jax.ShapeDtypeStruc...  2.72 us
    all_to_all x1, waiting for transfers between devices, exchange(): return lax.all_to_all(value, axes, split_axis=0, concat_axis=0, tiled=True)  2.68 us
  transfers between devices with their start and end apart: 6, of which 6 were waited for; matrix products, arithmetic and copies ran while one was open for 0% of the time, Pallas kernels for 3%

profile of v4, /device:TPU:1, one launch (start us, length us, event | category | flops | bytes accessed | tf_op | source)
XLA Modules:
  0.0 80.2 jit_solution(3472593275465752148)
XLA Ops:
  0.6 0.7 copy-done.1
  1.4 0.8 copy-done.3
  2.2 1.0 %transmission.1 = bf16[16,2,4,8,256]{4,3,2,1,0:T(8,128)(2,1)} custom-call(f32[4,8,256]{2,1,0:T(8,128)S(1)} %copy-done.1, f32[4,8,256]{2,1,0:T(8,128)S(1)} %copy-done.3), custom_call_target="tpu_custom_call" | custom-call | tf_op jit(solution)/shard_map/transmission/pallas_call | solution.py:47
  3.1 9.1 %all-to-all-start = ((bf16[16,2,4,8,256]{4,3,2,1,0:T(8,128)(2,1)}), bf16[16,2,4,8,256]{4,3,2,1,0:T(8,128)(2,1)S(1)}, u32[]{:S(2)}, u32[]{:S(2)}) async-start(bf16[16,2,4,8,256]{4,3,2,1,0:T(8,128)(2,1)} %transmission.1), calls=%async_computation | async-start | bytes 1048576 | tf_op jit(solution)/shard_map/all_to_all | solution.py:32
  12.3 2.7 %sweeps_and_waves.1 = (bf16[512,512]{1,0:T(8,128)(2,1)S(1)}, bf16[512,512]{1,0:T(8,128)(2,1)S(1)}, f32[2,2,256,256]{3,2,1,0:T(8,128)S(1)}) custom-call(s32[2,2]{1,0:T(2,128)S(1)} %copy-done.5), custom_call_target="tpu_custom_call" | custom-call | tf_op jit(solution)/shard_map/sweeps_and_waves/pallas_call | solution.py:93
  15.1 4.4 %collective-permute-start = (f32[2,4,8,256]{3,2,1,0:T(8,128)S(1)}, f32[2,4,8,256]{3,2,1,0:T(8,128)S(1)}, u32[]{:S(2)}, u32[]{:S(2)}) collective-permute-start(f32[2,4,8,256]{3,2,1,0:T(8,128)S(1)} %get-tuple-element.45), channel_id=1, source_target_pairs={{1,2},{3,4},{5,6},{7,8},{9,10},{11,12},{13,14},{15,16},{17,18},{19... | collective-permute-start | bytes 196616 | tf_op jit(solution)/shard_map/ppermute | solution.py:287
  19.5 0.1 copy.8
  19.7 2.2 %collective-permute-done = f32[2,4,8,256]{3,2,1,0:T(8,128)S(1)} collective-permute-done((f32[2,4,8,256]{3,2,1,0:T(8,128)S(1)}, f32[2,4,8,256]{3,2,1,0:T(8,128)S(1)}, u32[]{:S(2)}, u32[]{:S(2)}) %collective-permute-start) | collective-permute-done | bytes 65568 | tf_op jit(solution)/shard_map/ppermute | solution.py:287
  21.9 0.1 collective-permute-start.1
  22.1 1.2 %collective-permute-done.1 = f32[2,4,8,256]{3,2,1,0:T(8,128)S(1)} collective-permute-done((f32[2,4,8,256]{3,2,1,0:T(8,128)S(1)}, f32[2,4,8,256]{3,2,1,0:T(8,128)S(1)}, u32[]{:S(2)}, u32[]{:S(2)}) %collective-permute-start.1) | collective-permute-done | bytes 65568 | tf_op jit(solution)/shard_map/ppermute | solution.py:28
  23.4 2.7 %all-to-all-done.own = bf16[16,2,4,8,256]{4,3,2,1,0:T(8,128)(2,1)S(1)} async-done(((bf16[16,2,4,8,256]{4,3,2,1,0:T(8,128)(2,1)}), bf16[16,2,4,8,256]{4,3,2,1,0:T(8,128)(2,1)S(1)}, u32[]{:S(2)}, u32[]{:S(2)}) %all-to-all-start) | async-done | bytes 524320 | tf_op jit(solution)/shard_map/all_to_all | solution.py:32
  26.1 2.6 %collective-permute-start.2 = (bf16[16,2,4,8,256]{4,3,2,1,0:T(8,128)(2,1)S(1)}, bf16[16,2,4,8,256]{4,3,2,1,0:T(8,128)(2,1)S(1)}, u32[]{:S(2)}, u32[]{:S(2)}) collective-permute-start(bf16[16,2,4,8,256]{4,3,2,1,0:T(8,128)(2,1)S(1)} %all-to-all-done.own), channel_id=1, source_target_pairs={{0,1},{1,0},{2,3},{3,2},{4,5},{5,4},{6,7},{7,6},{8,9},{9,8},{10,11... | collective-permute-start | bytes 1572872 | tf_op jit(solution)/shard_map/ppermute | solution.py:28
  28.7 1.5 %collective-permute-done.2.other = bf16[16,2,4,8,256]{4,3,2,1,0:T(8,128)(2,1)S(1)} collective-permute-done((bf16[16,2,4,8,256]{4,3,2,1,0:T(8,128)(2,1)S(1)}, bf16[16,2,4,8,256]{4,3,2,1,0:T(8,128)(2,1)S(1)}, u32[]{:S(2)}, u32[]{:S(2)}) %collective-permute-start.2) | collective-permute-done | bytes 524320 | tf_op jit(solution)/shard_map/ppermute | solution.py:28
  30.2 2.7 %angles.1 = (bf16[4,4,4,24,256]{4,3,2,1,0:T(8,128)(2,1)S(1)}, bf16[4,4,4,24,256]{4,3,2,1,0:T(8,128)(2,1)S(1)}) custom-call(s32[6]{0:T(128)S(1)} %pad_add_fusion.1.numbers, bf16[16,2,4,8,256]{4,3,2,1,0:T(8,128)(2,1)S(1)} %all-to-all-done.own, bf16[16,2,4,8,256]{4,3,2,1,0:T(8,128)(2,1)S(1)} %collective-permute-done.2.other, ...), custom_call_target="tpu_custom_call" | custom-call | tf_op jit(solution)/shard_map/angles/pallas_call | solution.py:198
  33.0 0.5 collective-permute-start.3
  33.4 1.9 %collective-permute-done.3 = bf16[4,4,4,24,256]{4,3,2,1,0:T(8,128)(2,1)S(1)} collective-permute-done((bf16[4,4,4,24,256]{4,3,2,1,0:T(8,128)(2,1)S(1)}, bf16[4,4,4,24,256]{4,3,2,1,0:T(8,128)(2,1)S(1)}, u32[]{:S(2)}, u32[]{:S(2)}) %collective-permute-start.3) | collective-permute-done | bytes 786464 | tf_op jit(solution)/shard_map/ppermute | solution.py:28
  35.3 0.2 add_convert_fusion
  35.6 19.2 %all_to_all.15 = bf16[16,4,24,256]{3,2,1,0:T(8,128)(2,1)S(1)} all-to-all(bf16[16,4,24,256]{3,2,1,0:T(8,128)(2,1)S(1)} %bitcast.40), channel_id=1, replica_groups=mesh['y'=4,'zh'=2,'zl'=4,'x'=4,'c'=2] {'y','x'}, dimensions={0} | all-to-all | bytes 1572864 | tf_op jit(solution)/shard_map/all_to_all | solution.py:32
  54.8 0.1 reduce_sum.12
  54.9 17.6 %all_to_all.16.column = bf16[32,24,256]{2,1,0:T(8,128)(2,1)S(1)} all-to-all(bf16[32,24,256]{2,1,0:T(8,128)(2,1)S(1)} %bitcast.41), channel_id=1, replica_groups=mesh['y'=4,'zh'=2,'zl'=4,'x'=4,'c'=2] {'y','zh','zl'}, dimensions={0} | all-to-all | bytes 786432 | tf_op jit(solution)/shard_map/all_to_all | solution.py:32
  72.5 1.2 %regularize.1 = (f32[2,4,8,256]{3,2,1,0:T(8,128)S(1)}, f32[2,4,8,256]{3,2,1,0:T(8,128)S(1)}) custom-call(s32[6]{0:T(128)S(1)} %pad_add_fusion.1.numbers, bf16[32,24,256]{2,1,0:T(8,128)(2,1)S(1)} %all_to_all.16.column, f32[4,24,256]{2,1,0:T(8,128)S(1)} %pad_maximum_fusion.params), custom_call_target="tpu_custom_call" | custom-call | tf_op jit(solution)/shard_map/regularize/pallas_call | solution.py:261
  73.7 4.9 %collective-permute-start.4 = (f32[2,4,8,256]{3,2,1,0:T(8,128)S(1)}, f32[2,4,8,256]{3,2,1,0:T(8,128)S(1)}, u32[]{:S(2)}, u32[]{:S(2)}) collective-permute-start(f32[2,4,8,256]{3,2,1,0:T(8,128)S(1)} %get-tuple-element.37), channel_id=1, source_target_pairs={{0,1},{1,0},{2,3},{3,2},{4,5},{5,4},{6,7},{7,6},{8,9},{9,8},{10,11... | collective-permute-start | bytes 196616 | tf_op jit(solution)/shard_map/ppermute | solution.py:28
  78.6 0.9 %collective-permute-done.4 = f32[2,4,8,256]{3,2,1,0:T(8,128)S(1)} collective-permute-done((f32[2,4,8,256]{3,2,1,0:T(8,128)S(1)}, f32[2,4,8,256]{3,2,1,0:T(8,128)S(1)}, u32[]{:S(2)}, u32[]{:S(2)}) %collective-permute-start.4) | collective-permute-done | bytes 65568 | tf_op jit(solution)/shard_map/ppermute | solution.py:28
  79.5 0.7 fusion.3
  (26 shorter events, 0.4 us)
Async XLA Ops:
  0.6 0.8 copy-start.1
  1.4 0.8 copy-start.3
  2.1 10.1 %copy-start.5 = (s32[2,2]{1,0:T(2,128)S(1)}, s32[2,2]{1,0:T(2,128)}, u32[]{:S(2)}) copy-start(s32[2,2]{1,0:T(2,128)} %tilts) | copy-start | bytes 52
  2.2 12.9 %copy-start.2 = (f32[4,8,256]{2,1,0:T(8,128)S(1)}, f32[4,8,256]{2,1,0:T(8,128)}, u32[]{:S(2)}) copy-start(f32[4,8,256]{2,1,0:T(8,128)} %phase.1) | copy-start | bytes 98308
  2.2 12.9 %copy-start.4 = (f32[4,8,256]{2,1,0:T(8,128)S(1)}, f32[4,8,256]{2,1,0:T(8,128)}, u32[]{:S(2)}) copy-start(f32[4,8,256]{2,1,0:T(8,128)} %absorb.1) | copy-start | bytes 98308
  2.2 17.3 %copy-start.6 = (s32[2]{0:T(128)S(1)}, s32[2]{0:T(128)}, u32[]{:S(2)}) copy-start(s32[2]{0:T(128)} %param.10) | copy-start | bytes 28
  2.2 17.3 %copy-start.7 = (s32[2]{0:T(128)S(1)}, s32[2]{0:T(128)}, u32[]{:S(2)}) copy-start(s32[2]{0:T(128)} %param.9) | copy-start | bytes 28
  3.1 27.1 %copy-start = (bf16[2,2,256,256]{3,2,1,0:T(8,128)(2,1)S(1)}, bf16[2,2,256,256]{3,2,1,0:T(8,128)(2,1)}, u32[]{:S(2)}) copy-start(bf16[2,2,256,256]{3,2,1,0:T(8,128)(2,1)} %measured.1) | copy-start | bytes 1572868
  3.1 22.9 %all-to-all-start = ((bf16[16,2,4,8,256]{4,3,2,1,0:T(8,128)(2,1)}), bf16[16,2,4,8,256]{4,3,2,1,0:T(8,128)(2,1)S(1)}, u32[]{:S(2)}, u32[]{:S(2)}) async-start(bf16[16,2,4,8,256]{4,3,2,1,0:T(8,128)(2,1)} %transmission.1), calls=%async_computation | async-start | bytes 1048576 | tf_op jit(solution)/shard_map/all_to_all | solution.py:32
  15.1 6.9 %collective-permute-start = (f32[2,4,8,256]{3,2,1,0:T(8,128)S(1)}, f32[2,4,8,256]{3,2,1,0:T(8,128)S(1)}, u32[]{:S(2)}, u32[]{:S(2)}) collective-permute-start(f32[2,4,8,256]{3,2,1,0:T(8,128)S(1)} %get-tuple-element.45), channel_id=1, source_target_pairs={{1,2},{3,4},{5,6},{7,8},{9,10},{11,12},{13,14},{15,16},{17,18},{19... | collective-permute-start | bytes 196616 | tf_op jit(solution)/shard_map/ppermute | solution.py:287
  21.9 1.3 %collective-permute-start.1 = (f32[2,4,8,256]{3,2,1,0:T(8,128)S(1)}, f32[2,4,8,256]{3,2,1,0:T(8,128)S(1)}, u32[]{:S(2)}, u32[]{:S(2)}) collective-permute-start(f32[2,4,8,256]{3,2,1,0:T(8,128)S(1)} %select_bitcast_fusion.2), channel_id=1, source_target_pairs={{0,1},{1,0},{2,3},{3,2},{4,5},{5,4},{6,7},{7,6},{8,9},{9,8},{10,11... | collective-permute-start | bytes 196616 | tf_op jit(solution)/shard_map/ppermute | solution.py:28
  26.1 4.2 %collective-permute-start.2 = (bf16[16,2,4,8,256]{4,3,2,1,0:T(8,128)(2,1)S(1)}, bf16[16,2,4,8,256]{4,3,2,1,0:T(8,128)(2,1)S(1)}, u32[]{:S(2)}, u32[]{:S(2)}) collective-permute-start(bf16[16,2,4,8,256]{4,3,2,1,0:T(8,128)(2,1)S(1)} %all-to-all-done.own), channel_id=1, source_target_pairs={{0,1},{1,0},{2,3},{3,2},{4,5},{5,4},{6,7},{7,6},{8,9},{9,8},{10,11... | collective-permute-start | bytes 1572872 | tf_op jit(solution)/shard_map/ppermute | solution.py:28
  33.0 2.4 %collective-permute-start.3 = (bf16[4,4,4,24,256]{4,3,2,1,0:T(8,128)(2,1)S(1)}, bf16[4,4,4,24,256]{4,3,2,1,0:T(8,128)(2,1)S(1)}, u32[]{:S(2)}, u32[]{:S(2)}) collective-permute-start(bf16[4,4,4,24,256]{4,3,2,1,0:T(8,128)(2,1)S(1)} %get-tuple-element.34), channel_id=1, source_target_pairs={{0,1},{1,0},{2,3},{3,2},{4,5},{5,4},{6,7},{7,6},{8,9},{9,8},{10,11... | collective-permute-start | bytes 2359304 | tf_op jit(solution)/shard_map/ppermute | solution.py:28
  73.7 5.8 %collective-permute-start.4 = (f32[2,4,8,256]{3,2,1,0:T(8,128)S(1)}, f32[2,4,8,256]{3,2,1,0:T(8,128)S(1)}, u32[]{:S(2)}, u32[]{:S(2)}) collective-permute-start(f32[2,4,8,256]{3,2,1,0:T(8,128)S(1)} %get-tuple-element.37), channel_id=1, source_target_pairs={{0,1},{1,0},{2,3},{3,2},{4,5},{5,4},{6,7},{7,6},{8,9},{9,8},{10,11... | collective-permute-start | bytes 196616 | tf_op jit(solution)/shard_map/ppermute | solution.py:28

commit v5 on v4

--- a/solution.py
+++ b/solution.py
@@ -32,9 +32,9 @@
     return lax.all_to_all(value, axes, split_axis=0, concat_axis=0, tiled=True)
 
 
-def outgoing_kernel(phase, absorb, out):
-    decay = jnp.exp(-absorb[...])
-    angle = phase[...]
+def outgoing_kernel(params, out):
+    decay = jnp.exp(-params[1])
+    angle = params[0]
     real = (decay * jnp.cos(angle)).astype(jnp.bfloat16)
     imag = (decay * jnp.sin(angle)).astype(jnp.bfloat16)
     for chip in range(out.shape[0]):
@@ -42,16 +42,16 @@
         out[chip, 1] = imag
 
 
-def outgoing(phase, absorb, chips):
+def outgoing(params, chips):
     vmem = pl.BlockSpec(memory_space=pltpu.VMEM)
     return pl.pallas_call(
         outgoing_kernel,
-        out_shape=jax.ShapeDtypeStruct((chips, 2, *phase.shape), jnp.bfloat16),
-        in_specs=[vmem] * 2,
+        out_shape=jax.ShapeDtypeStruct((chips, *params.shape), jnp.bfloat16),
+        in_specs=[vmem],
         out_specs=vmem,
         compiler_params=pltpu.CompilerParams(vmem_limit_bytes=4 << 20),
         name="transmission",
-    )(phase, absorb)
+    )(params)
 
 
 def setup_kernel(tilts, forward, backward, waves):
@@ -165,7 +165,7 @@
         back_imag = back[span(slot), length:]
         terms[0, 3 * slot] = enter_real * back_imag - enter_imag * back_real
         terms[1, 3 * slot] = -(enter_real * back_real + enter_imag * back_imag)
-    depth, columns, blocks, _, _ = keep.shape
+    blocks, columns, depth, _, _ = keep.shape
     strip = own.shape[3]
     near = lax.broadcasted_iota(jnp.int32, (strip, length), 0) < strip // 2
     for out, component in ((keep, core), (send, 1 - core)):
@@ -185,7 +185,7 @@
                         near, plane[after : after + strip], plane[before : before + strip]
                     )
                     rows = jnp.concatenate([plane[start : start + 2 * strip], border], 0)
-                    out[level, column, block] = rows.astype(jnp.bfloat16)
+                    out[block, column, level] = rows.astype(jnp.bfloat16)
 
 
 def angles(numbers, own, other, forward, backward, waves, measured):
@@ -194,7 +194,7 @@
     slots = measured.shape[1]
     zl, x = SIZES[2], SIZES[3]
     vmem = pl.BlockSpec(memory_space=pltpu.VMEM)
-    half = jax.ShapeDtypeStruct((depth, x, zl, 3 * own.shape[3], length), jnp.bfloat16)
+    half = jax.ShapeDtypeStruct((zl, x, depth, 3 * own.shape[3], length), jnp.bfloat16)
     return pl.pallas_call(
         angles_kernel,
         out_shape=(half, half),
@@ -213,7 +213,7 @@
 
 def regularize_kernel(numbers, column, params, mine, other, *, norm):
     depth, ring, length = params.shape
-    owners = column.shape[0] // depth
+    parts = column.shape[0] // depth
     strip = mine.shape[2]
     mine_first = numbers[0] == 0
     index = lax.broadcasted_iota(jnp.int32, (ring, length), 0)
@@ -229,10 +229,8 @@
         return start + LAMBDA_TV * (dual_rows - above + dual_cols - left)
 
     for level in range(depth):
-        gradient = column[level * owners].astype(jnp.float32)
-        for owner in range(1, owners):
-            gradient = gradient + column[level * owners + owner].astype(jnp.float32)
-        gradient = gradient * norm
+        pieces = [column[level * parts + part] for part in range(parts)]
+        gradient = jnp.concatenate(pieces, 1).astype(jnp.float32) * norm
         start = params[level] - STEP_SIZE * gradient
         primal = start
         dual_rows = dual_cols = None
@@ -275,12 +273,12 @@
     core = lax.axis_index("c")
     mine_first = core == 0
 
-    sent = outgoing(phase, absorb, chips)
+    params = lax.optimization_barrier(jnp.stack([phase, absorb]))
+    sent = outgoing(params, chips)
     sent, tilts = lax.optimization_barrier((sent, tilts))
     own = exchange(sent, CHIPS)
     forward_sweep, backward_sweep, waves = setup(tilts, length)
-    phase, absorb, waves = lax.optimization_barrier((phase, absorb, waves))
-    params = jnp.stack([phase, absorb])
+    params, waves = lax.optimization_barrier((params, waves))
     tiles = 2 * chips
     borders = [(i, i + 1) for i in range(1, tiles - 1, 2)]
     borders = borders + [(j, i) for i, j in borders]
@@ -306,12 +304,13 @@
     keep, send = angles(numbers, own, other, forward_sweep, backward_sweep, waves, measured)
 
     pair = keep.astype(jnp.float32) + swap_cores(send).astype(jnp.float32)
-    y, x = SIZES[0], SIZES[3]
-    pair = pair.astype(jnp.bfloat16).reshape(y * x, -1, *keep.shape[-2:])
-    plane = exchange(pair, ("y", "x")).astype(jnp.float32).sum(0).astype(jnp.bfloat16)
+    pair = pair.astype(jnp.bfloat16).reshape(chips, *keep.shape[2:])
+    plane = exchange(pair, CHIPS).astype(jnp.float32).sum(0).astype(jnp.bfloat16)
     copies = SIZES[0] * SIZES[1]
-    sent = jnp.broadcast_to(plane[None], (copies, *plane.shape)).reshape(-1, *plane.shape[1:])
-    column = exchange(sent, ("y", "zh", "zl"))
+    parts = copies // depth
+    pieces = jnp.stack(jnp.split(plane, parts, 2), 1).reshape(copies, plane.shape[1], -1)
+    piece = exchange(pieces, ANG).astype(jnp.float32).sum(0).astype(jnp.bfloat16)
+    column = exchange(jnp.broadcast_to(piece[None], (copies, *piece.shape)), ANG)
     all_slots = slots * math.prod(SIZES)
     mine, theirs = regularize(numbers, column, ring, 1.0 / math.sqrt(all_slots))
     theirs = swap_cores(theirs)

time: 80.6 us -> 96.7 us (1.20)
  blocking collectives: 36.8 us -> 53.6 us
  local copies, waits for them, and re-layouts: 1.74 us -> 0.22 us
    all_to_all x2 -> x3, blocking collectives: 36.8 us -> 53.6 us  [exchange(): return lax.all_to_all(value, axes, split_axis=0, concat_axis=0, tiled=True)]
    unnamed x16 -> x8, local copies, waits for them, and re-layouts: 1.53 us -> 0.02 us
where the time goes in v5:
time: 96.7 us; the launch traced here: 96.3 us
  blocking collectives  53.6 us (55%)
  starting transfers between devices  21.6 us (22%)
  waiting for transfers between devices  10.5 us (11%)
  Pallas kernels  7.53 us (8%)
  other arithmetic  2.05 us (2%)
    all_to_all x3, blocking collectives, exchange(): return lax.all_to_all(value, axes, split_axis=0, concat_axis=0, tiled=True)  53.6 us
    all_to_all x1, starting transfers between devices, exchange(): return lax.all_to_all(value, axes, split_axis=0, concat_axis=0, tiled=True)  9.15 us
    ppermute x4, starting transfers between devices, swap_cores(): return lax.ppermute(value, 'c', [(0, 1), (1, 0)])  8.07 us
    ppermute x4, waiting for transfers between devices, swap_cores(): return lax.ppermute(value, 'c', [(0, 1), (1, 0)])  5.51 us
    ppermute x1, starting transfers between devices, on_device(): near = jnp.stack([params, lax.ppermute(params, TILE, borders)])  4.39 us
    pallas_call x1, Pallas kernels, angles(): pl.pallas_call(angles_kernel, out_shape=(half, half), in_specs=[pl.BlockS...  2.72 us
    pallas_call x1, Pallas kernels, setup(): pl.pallas_call(setup_kernel, out_shape=(sweep, sweep, jax.ShapeDtypeStruc...  2.72 us
    all_to_all x1, waiting for transfers between devices, exchange(): return lax.all_to_all(value, axes, split_axis=0, concat_axis=0, tiled=True)  2.68 us
  transfers between devices with their start and end apart: 6, of which 6 were waited for; matrix products, arithmetic and copies ran while one was open for 0% of the time, Pallas kernels for 3%

profile of v5, /device:TPU:1, one launch (start us, length us, event | category | flops | bytes accessed | tf_op | source)
XLA Modules:
  0.0 96.3 jit_solution(1282900123066955448)
XLA Ops:
  0.7 0.8 pad_maximum_fusion.3.params
  1.5 1.0 transmission.1
  2.4 9.1 %all-to-all-start = ((bf16[16,2,4,8,256]{4,3,2,1,0:T(8,128)(2,1)}), bf16[16,2,4,8,256]{4,3,2,1,0:T(8,128)(2,1)S(1)}, u32[]{:S(2)}, u32[]{:S(2)}) async-start(bf16[16,2,4,8,256]{4,3,2,1,0:T(8,128)(2,1)} %transmission.1), calls=%async_computation | async-start | bytes 1048576 | tf_op jit(solution)/shard_map/all_to_all | solution.py:32
  11.6 2.7 %sweeps_and_waves.1 = (bf16[512,512]{1,0:T(8,128)(2,1)S(1)}, bf16[512,512]{1,0:T(8,128)(2,1)S(1)}, f32[2,2,256,256]{3,2,1,0:T(8,128)S(1)}) custom-call(s32[2,2]{1,0:T(2,128)S(1)} %copy-done.1), custom_call_target="tpu_custom_call" | custom-call | tf_op jit(solution)/shard_map/sweeps_and_waves/pallas_call | solution.py:93
  14.3 4.4 %collective-permute-start = (f32[2,4,8,256]{3,2,1,0:T(8,128)S(1)}, f32[2,4,8,256]{3,2,1,0:T(8,128)S(1)}, u32[]{:S(2)}, u32[]{:S(2)}) collective-permute-start(f32[2,4,8,256]{3,2,1,0:T(8,128)S(1)} %pad_maximum_fusion.3.params), channel_id=1, source_target_pairs={{1,2},{3,4},{5,6},{7,8},{9,10},{11,12},{13,14},{15,16},{17,18},{19... | collective-permute-start | bytes 196616 | tf_op jit(solution)/shard_map/ppermute | solution.py:285
  18.7 0.1 copy.10
  18.9 2.3 %collective-permute-done = f32[2,4,8,256]{3,2,1,0:T(8,128)S(1)} collective-permute-done((f32[2,4,8,256]{3,2,1,0:T(8,128)S(1)}, f32[2,4,8,256]{3,2,1,0:T(8,128)S(1)}, u32[]{:S(2)}, u32[]{:S(2)}) %collective-permute-start) | collective-permute-done | bytes 65568 | tf_op jit(solution)/shard_map/ppermute | solution.py:285
  21.2 0.1 collective-permute-start.1
  21.4 1.2 %collective-permute-done.1 = f32[2,4,8,256]{3,2,1,0:T(8,128)S(1)} collective-permute-done((f32[2,4,8,256]{3,2,1,0:T(8,128)S(1)}, f32[2,4,8,256]{3,2,1,0:T(8,128)S(1)}, u32[]{:S(2)}, u32[]{:S(2)}) %collective-permute-start.1) | collective-permute-done | bytes 65568 | tf_op jit(solution)/shard_map/ppermute | solution.py:28
  22.7 2.7 %all-to-all-done.own = bf16[16,2,4,8,256]{4,3,2,1,0:T(8,128)(2,1)S(1)} async-done(((bf16[16,2,4,8,256]{4,3,2,1,0:T(8,128)(2,1)}), bf16[16,2,4,8,256]{4,3,2,1,0:T(8,128)(2,1)S(1)}, u32[]{:S(2)}, u32[]{:S(2)}) %all-to-all-start) | async-done | bytes 524320 | tf_op jit(solution)/shard_map/all_to_all | solution.py:32
  25.3 2.6 %collective-permute-start.2 = (bf16[16,2,4,8,256]{4,3,2,1,0:T(8,128)(2,1)S(1)}, bf16[16,2,4,8,256]{4,3,2,1,0:T(8,128)(2,1)S(1)}, u32[]{:S(2)}, u32[]{:S(2)}) collective-permute-start(bf16[16,2,4,8,256]{4,3,2,1,0:T(8,128)(2,1)S(1)} %all-to-all-done.own), channel_id=1, source_target_pairs={{0,1},{1,0},{2,3},{3,2},{4,5},{5,4},{6,7},{7,6},{8,9},{9,8},{10,11... | collective-permute-start | bytes 1572872 | tf_op jit(solution)/shard_map/ppermute | solution.py:28
  28.0 1.5 %collective-permute-done.2.other = bf16[16,2,4,8,256]{4,3,2,1,0:T(8,128)(2,1)S(1)} collective-permute-done((bf16[16,2,4,8,256]{4,3,2,1,0:T(8,128)(2,1)S(1)}, bf16[16,2,4,8,256]{4,3,2,1,0:T(8,128)(2,1)S(1)}, u32[]{:S(2)}, u32[]{:S(2)}) %collective-permute-start.2) | collective-permute-done | bytes 524320 | tf_op jit(solution)/shard_map/ppermute | solution.py:28
  29.5 2.7 %angles.1 = (bf16[4,4,4,24,256]{4,3,2,1,0:T(8,128)(2,1)S(1)}, bf16[4,4,4,24,256]{4,3,2,1,0:T(8,128)(2,1)S(1)}) custom-call(s32[6]{0:T(128)S(1)} %pad_add_fusion.1.numbers, bf16[16,2,4,8,256]{4,3,2,1,0:T(8,128)(2,1)S(1)} %all-to-all-done.own, bf16[16,2,4,8,256]{4,3,2,1,0:T(8,128)(2,1)S(1)} %collective-permute-done.2.other, ...), custom_call_target="tpu_custom_call" | custom-call | tf_op jit(solution)/shard_map/angles/pallas_call | solution.py:198
  32.2 0.5 collective-permute-start.3
  32.7 1.9 %collective-permute-done.3 = bf16[4,4,4,24,256]{4,3,2,1,0:T(8,128)(2,1)S(1)} collective-permute-done((bf16[4,4,4,24,256]{4,3,2,1,0:T(8,128)(2,1)S(1)}, bf16[4,4,4,24,256]{4,3,2,1,0:T(8,128)(2,1)S(1)}, u32[]{:S(2)}, u32[]{:S(2)}) %collective-permute-start.3) | collective-permute-done | bytes 786464 | tf_op jit(solution)/shard_map/ppermute | solution.py:28
  34.6 0.2 add_convert_fusion
  34.9 25.2 %all_to_all.20 = bf16[16,4,24,256]{3,2,1,0:T(8,128)(2,1)S(1)} all-to-all(bf16[16,4,24,256]{3,2,1,0:T(8,128)(2,1)S(1)} %bitcast.45), channel_id=1, replica_groups=mesh['y'=4,'zh'=2,'zl'=4,'x'=4,'c'=2] {'zl','x'}, dimensions={0} | all-to-all | bytes 1572864 | tf_op jit(solution)/shard_map/all_to_all | solution.py:32
  60.1 0.1 reduce_sum.24
  60.2 17.0 %all_to_all.21 = bf16[8,24,128]{2,1,0:T(8,128)(2,1)S(1)} all-to-all(bf16[8,24,128]{2,1,0:T(8,128)(2,1)S(1)} %bitcast.48), channel_id=1, replica_groups=mesh['y'=4,'zh'=2,'zl'=4,'x'=4,'c'=2] {'y','zh'}, dimensions={0} | all-to-all | bytes 98304 | tf_op jit(solution)/shard_map/all_to_all | solution.py:32
  77.2 11.4 %all_to_all.22.column = bf16[8,24,128]{2,1,0:T(8,128)(2,1)S(1)} all-to-all(bf16[8,24,128]{2,1,0:T(8,128)(2,1)S(1)} %broadcast_in_dim.24), channel_id=1, replica_groups=mesh['y'=4,'zh'=2,'zl'=4,'x'=4,'c'=2] {'y','zh'}, dimensions={0} | all-to-all | bytes 98304 | tf_op jit(solution)/shard_map/all_to_all | solution.py:32
  88.7 1.1 %regularize.1 = (f32[2,4,8,256]{3,2,1,0:T(8,128)S(1)}, f32[2,4,8,256]{3,2,1,0:T(8,128)S(1)}) custom-call(s32[6]{0:T(128)S(1)} %pad_add_fusion.1.numbers, bf16[8,24,128]{2,1,0:T(8,128)(2,1)S(1)} %all_to_all.22.column, f32[4,24,256]{2,1,0:T(8,128)S(1)} %pad_maximum_fusion.params), custom_call_target="tpu_custom_call" | custom-call | tf_op jit(solution)/shard_map/regularize/pallas_call | solution.py:259
  89.8 4.9 %collective-permute-start.4 = (f32[2,4,8,256]{3,2,1,0:T(8,128)S(1)}, f32[2,4,8,256]{3,2,1,0:T(8,128)S(1)}, u32[]{:S(2)}, u32[]{:S(2)}) collective-permute-start(f32[2,4,8,256]{3,2,1,0:T(8,128)S(1)} %get-tuple-element.35), channel_id=1, source_target_pairs={{0,1},{1,0},{2,3},{3,2},{4,5},{5,4},{6,7},{7,6},{8,9},{9,8},{10,11... | collective-permute-start | bytes 196616 | tf_op jit(solution)/shard_map/ppermute | solution.py:28
  94.7 0.9 collective-permute-done.4
  95.6 0.7 fusion.3
  (22 shorter events, 0.4 us)
Async XLA Ops:
  0.6 10.9 %copy-start.1 = (s32[2,2]{1,0:T(2,128)S(1)}, s32[2,2]{1,0:T(2,128)}, u32[]{:S(2)}) copy-start(s32[2,2]{1,0:T(2,128)} %tilts) | copy-start | bytes 52
  0.6 18.1 %copy-start.2 = (s32[2]{0:T(128)S(1)}, s32[2]{0:T(128)}, u32[]{:S(2)}) copy-start(s32[2]{0:T(128)} %param.10) | copy-start | bytes 28
  0.7 18.1 %copy-start.3 = (s32[2]{0:T(128)S(1)}, s32[2]{0:T(128)}, u32[]{:S(2)}) copy-start(s32[2]{0:T(128)} %param.9) | copy-start | bytes 28
  2.4 27.1 %copy-start = (bf16[2,2,256,256]{3,2,1,0:T(8,128)(2,1)S(1)}, bf16[2,2,256,256]{3,2,1,0:T(8,128)(2,1)}, u32[]{:S(2)}) copy-start(bf16[2,2,256,256]{3,2,1,0:T(8,128)(2,1)} %measured.1) | copy-start | bytes 1572868
  2.4 22.9 %all-to-all-start = ((bf16[16,2,4,8,256]{4,3,2,1,0:T(8,128)(2,1)}), bf16[16,2,4,8,256]{4,3,2,1,0:T(8,128)(2,1)S(1)}, u32[]{:S(2)}, u32[]{:S(2)}) async-start(bf16[16,2,4,8,256]{4,3,2,1,0:T(8,128)(2,1)} %transmission.1), calls=%async_computation | async-start | bytes 1048576 | tf_op jit(solution)/shard_map/all_to_all | solution.py:32
  14.3 6.9 %collective-permute-start = (f32[2,4,8,256]{3,2,1,0:T(8,128)S(1)}, f32[2,4,8,256]{3,2,1,0:T(8,128)S(1)}, u32[]{:S(2)}, u32[]{:S(2)}) collective-permute-start(f32[2,4,8,256]{3,2,1,0:T(8,128)S(1)} %pad_maximum_fusion.3.params), channel_id=1, source_target_pairs={{1,2},{3,4},{5,6},{7,8},{9,10},{11,12},{13,14},{15,16},{17,18},{19... | collective-permute-start | bytes 196616 | tf_op jit(solution)/shard_map/ppermute | solution.py:285
  21.2 1.3 %collective-permute-start.1 = (f32[2,4,8,256]{3,2,1,0:T(8,128)S(1)}, f32[2,4,8,256]{3,2,1,0:T(8,128)S(1)}, u32[]{:S(2)}, u32[]{:S(2)}) collective-permute-start(f32[2,4,8,256]{3,2,1,0:T(8,128)S(1)} %select_bitcast_fusion.2), channel_id=1, source_target_pairs={{0,1},{1,0},{2,3},{3,2},{4,5},{5,4},{6,7},{7,6},{8,9},{9,8},{10,11... | collective-permute-start | bytes 196616 | tf_op jit(solution)/shard_map/ppermute | solution.py:28
  25.3 4.2 %collective-permute-start.2 = (bf16[16,2,4,8,256]{4,3,2,1,0:T(8,128)(2,1)S(1)}, bf16[16,2,4,8,256]{4,3,2,1,0:T(8,128)(2,1)S(1)}, u32[]{:S(2)}, u32[]{:S(2)}) collective-permute-start(bf16[16,2,4,8,256]{4,3,2,1,0:T(8,128)(2,1)S(1)} %all-to-all-done.own), channel_id=1, source_target_pairs={{0,1},{1,0},{2,3},{3,2},{4,5},{5,4},{6,7},{7,6},{8,9},{9,8},{10,11... | collective-permute-start | bytes 1572872 | tf_op jit(solution)/shard_map/ppermute | solution.py:28
  32.2 2.4 %collective-permute-start.3 = (bf16[4,4,4,24,256]{4,3,2,1,0:T(8,128)(2,1)S(1)}, bf16[4,4,4,24,256]{4,3,2,1,0:T(8,128)(2,1)S(1)}, u32[]{:S(2)}, u32[]{:S(2)}) collective-permute-start(bf16[4,4,4,24,256]{4,3,2,1,0:T(8,128)(2,1)S(1)} %get-tuple-element.32), channel_id=1, source_target_pairs={{0,1},{1,0},{2,3},{3,2},{4,5},{5,4},{6,7},{7,6},{8,9},{9,8},{10,11... | collective-permute-start | bytes 2359304 | tf_op jit(solution)/shard_map/ppermute | solution.py:28
  89.8 5.8 %collective-permute-start.4 = (f32[2,4,8,256]{3,2,1,0:T(8,128)S(1)}, f32[2,4,8,256]{3,2,1,0:T(8,128)S(1)}, u32[]{:S(2)}, u32[]{:S(2)}) collective-permute-start(f32[2,4,8,256]{3,2,1,0:T(8,128)S(1)} %get-tuple-element.35), channel_id=1, source_target_pairs={{0,1},{1,0},{2,3},{3,2},{4,5},{5,4},{6,7},{7,6},{8,9},{9,8},{10,11... | collective-permute-start | bytes 196616 | tf_op jit(solution)/shard_map/ppermute | solution.py:28

commit v6 on v4

--- a/solution.py
+++ b/solution.py
@@ -32,9 +32,9 @@
     return lax.all_to_all(value, axes, split_axis=0, concat_axis=0, tiled=True)
 
 
-def outgoing_kernel(phase, absorb, out):
-    decay = jnp.exp(-absorb[...])
-    angle = phase[...]
+def outgoing_kernel(params, out):
+    decay = jnp.exp(-params[1])
+    angle = params[0]
     real = (decay * jnp.cos(angle)).astype(jnp.bfloat16)
     imag = (decay * jnp.sin(angle)).astype(jnp.bfloat16)
     for chip in range(out.shape[0]):
@@ -42,16 +42,16 @@
         out[chip, 1] = imag
 
 
-def outgoing(phase, absorb, chips):
+def outgoing(params, chips):
     vmem = pl.BlockSpec(memory_space=pltpu.VMEM)
     return pl.pallas_call(
         outgoing_kernel,
-        out_shape=jax.ShapeDtypeStruct((chips, 2, *phase.shape), jnp.bfloat16),
-        in_specs=[vmem] * 2,
+        out_shape=jax.ShapeDtypeStruct((chips, *params.shape), jnp.bfloat16),
+        in_specs=[vmem],
         out_specs=vmem,
         compiler_params=pltpu.CompilerParams(vmem_limit_bytes=4 << 20),
         name="transmission",
-    )(phase, absorb)
+    )(params)
 
 
 def setup_kernel(tilts, forward, backward, waves):
@@ -275,12 +275,12 @@
     core = lax.axis_index("c")
     mine_first = core == 0
 
-    sent = outgoing(phase, absorb, chips)
+    params = lax.optimization_barrier(jnp.stack([phase, absorb]))
+    sent = outgoing(params, chips)
     sent, tilts = lax.optimization_barrier((sent, tilts))
     own = exchange(sent, CHIPS)
     forward_sweep, backward_sweep, waves = setup(tilts, length)
-    phase, absorb, waves = lax.optimization_barrier((phase, absorb, waves))
-    params = jnp.stack([phase, absorb])
+    params, waves = lax.optimization_barrier((params, waves))
     tiles = 2 * chips
     borders = [(i, i + 1) for i in range(1, tiles - 1, 2)]
     borders = borders + [(j, i) for i, j in borders]

time: 80.6 us -> 79.8 us (0.990)
  local copies, waits for them, and re-layouts: 1.74 us -> 0.23 us
    unnamed x16 -> x8, local copies, waits for them, and re-layouts: 1.53 us -> 0.02 us
where the time goes in v6:
time: 79.8 us; the launch traced here: 79.5 us
  blocking collectives  36.8 us (46%)
  starting transfers between devices  21.6 us (27%)
  waiting for transfers between devices  10.5 us (13%)
  Pallas kernels  7.54 us (9%)
  other arithmetic  2.03 us (3%)
    all_to_all x2, blocking collectives, exchange(): return lax.all_to_all(value, axes, split_axis=0, concat_axis=0, tiled=True)  36.8 us
    all_to_all x1, starting transfers between devices, exchange(): return lax.all_to_all(value, axes, split_axis=0, concat_axis=0, tiled=True)  9.15 us
    ppermute x4, starting transfers between devices, swap_cores(): return lax.ppermute(value, 'c', [(0, 1), (1, 0)])  8.09 us
    ppermute x4, waiting for transfers between devices, swap_cores(): return lax.ppermute(value, 'c', [(0, 1), (1, 0)])  5.51 us
    ppermute x1, starting transfers between devices, on_device(): near = jnp.stack([params, lax.ppermute(params, TILE, borders)])  4.39 us
    pallas_call x1, Pallas kernels, setup(): pl.pallas_call(setup_kernel, out_shape=(sweep, sweep, jax.ShapeDtypeStruc...  2.72 us
    pallas_call x1, Pallas kernels, angles(): pl.pallas_call(angles_kernel, out_shape=(half, half), in_specs=[pl.BlockS...  2.72 us
    all_to_all x1, waiting for transfers between devices, exchange(): return lax.all_to_all(value, axes, split_axis=0, concat_axis=0, tiled=True)  2.68 us
  transfers between devices with their start and end apart: 6, of which 6 were waited for; matrix products, arithmetic and copies ran while one was open for 0% of the time, Pallas kernels for 3%

profile of v6, /device:TPU:1, one launch (start us, length us, event | category | flops | bytes accessed | tf_op | source)
XLA Modules:
  0.0 79.5 jit_solution(3321310336788357363)
XLA Ops:
  0.7 0.8 %pad_maximum_fusion.3.params = f32[2,4,8,256]{3,2,1,0:T(8,128)S(1)} fusion(f32[1,4,8,256]{3,2,1,0:T(8,128)} %bitcast.43, f32[1,4,8,256]{3,2,1,0:T(8,128)} %bitcast.44), kind=kLoop, calls=%fused_computation.12 | loop fusion | flops 16384 | bytes 131072 | tf_op jit(solution)/shard_map/stack | solution.py:278
  1.5 0.9 %transmission.1 = bf16[16,2,4,8,256]{4,3,2,1,0:T(8,128)(2,1)} custom-call(f32[2,4,8,256]{3,2,1,0:T(8,128)S(1)} %pad_maximum_fusion.3.params), custom_call_target="tpu_custom_call" | custom-call | tf_op jit(solution)/shard_map/transmission/pallas_call | solution.py:47
  2.4 9.1 %all-to-all-start = ((bf16[16,2,4,8,256]{4,3,2,1,0:T(8,128)(2,1)}), bf16[16,2,4,8,256]{4,3,2,1,0:T(8,128)(2,1)S(1)}, u32[]{:S(2)}, u32[]{:S(2)}) async-start(bf16[16,2,4,8,256]{4,3,2,1,0:T(8,128)(2,1)} %transmission.1), calls=%async_computation | async-start | bytes 1048576 | tf_op jit(solution)/shard_map/all_to_all | solution.py:32
  11.6 2.7 %sweeps_and_waves.1 = (bf16[512,512]{1,0:T(8,128)(2,1)S(1)}, bf16[512,512]{1,0:T(8,128)(2,1)S(1)}, f32[2,2,256,256]{3,2,1,0:T(8,128)S(1)}) custom-call(s32[2,2]{1,0:T(2,128)S(1)} %copy-done.1), custom_call_target="tpu_custom_call" | custom-call | tf_op jit(solution)/shard_map/sweeps_and_waves/pallas_call | solution.py:93
  14.3 4.4 %collective-permute-start = (f32[2,4,8,256]{3,2,1,0:T(8,128)S(1)}, f32[2,4,8,256]{3,2,1,0:T(8,128)S(1)}, u32[]{:S(2)}, u32[]{:S(2)}) collective-permute-start(f32[2,4,8,256]{3,2,1,0:T(8,128)S(1)} %pad_maximum_fusion.3.params), channel_id=1, source_target_pairs={{1,2},{3,4},{5,6},{7,8},{9,10},{11,12},{13,14},{15,16},{17,18},{19... | collective-permute-start | bytes 196616 | tf_op jit(solution)/shard_map/ppermute | solution.py:287
  18.7 0.1 copy.8
  18.8 0.1 reshape.22
  18.9 2.3 %collective-permute-done = f32[2,4,8,256]{3,2,1,0:T(8,128)S(1)} collective-permute-done((f32[2,4,8,256]{3,2,1,0:T(8,128)S(1)}, f32[2,4,8,256]{3,2,1,0:T(8,128)S(1)}, u32[]{:S(2)}, u32[]{:S(2)}) %collective-permute-start) | collective-permute-done | bytes 65568 | tf_op jit(solution)/shard_map/ppermute | solution.py:287
  21.2 0.1 collective-permute-start.1
  21.4 1.2 %collective-permute-done.1 = f32[2,4,8,256]{3,2,1,0:T(8,128)S(1)} collective-permute-done((f32[2,4,8,256]{3,2,1,0:T(8,128)S(1)}, f32[2,4,8,256]{3,2,1,0:T(8,128)S(1)}, u32[]{:S(2)}, u32[]{:S(2)}) %collective-permute-start.1) | collective-permute-done | bytes 65568 | tf_op jit(solution)/shard_map/ppermute | solution.py:28
  22.7 2.7 %all-to-all-done.own = bf16[16,2,4,8,256]{4,3,2,1,0:T(8,128)(2,1)S(1)} async-done(((bf16[16,2,4,8,256]{4,3,2,1,0:T(8,128)(2,1)}), bf16[16,2,4,8,256]{4,3,2,1,0:T(8,128)(2,1)S(1)}, u32[]{:S(2)}, u32[]{:S(2)}) %all-to-all-start) | async-done | bytes 524320 | tf_op jit(solution)/shard_map/all_to_all | solution.py:32
  25.3 2.6 %collective-permute-start.2 = (bf16[16,2,4,8,256]{4,3,2,1,0:T(8,128)(2,1)S(1)}, bf16[16,2,4,8,256]{4,3,2,1,0:T(8,128)(2,1)S(1)}, u32[]{:S(2)}, u32[]{:S(2)}) collective-permute-start(bf16[16,2,4,8,256]{4,3,2,1,0:T(8,128)(2,1)S(1)} %all-to-all-done.own), channel_id=1, source_target_pairs={{0,1},{1,0},{2,3},{3,2},{4,5},{5,4},{6,7},{7,6},{8,9},{9,8},{10,11... | collective-permute-start | bytes 1572872 | tf_op jit(solution)/shard_map/ppermute | solution.py:28
  28.0 1.5 %collective-permute-done.2.other = bf16[16,2,4,8,256]{4,3,2,1,0:T(8,128)(2,1)S(1)} collective-permute-done((bf16[16,2,4,8,256]{4,3,2,1,0:T(8,128)(2,1)S(1)}, bf16[16,2,4,8,256]{4,3,2,1,0:T(8,128)(2,1)S(1)}, u32[]{:S(2)}, u32[]{:S(2)}) %collective-permute-start.2) | collective-permute-done | bytes 524320 | tf_op jit(solution)/shard_map/ppermute | solution.py:28
  29.5 2.7 %angles.1 = (bf16[4,4,4,24,256]{4,3,2,1,0:T(8,128)(2,1)S(1)}, bf16[4,4,4,24,256]{4,3,2,1,0:T(8,128)(2,1)S(1)}) custom-call(s32[6]{0:T(128)S(1)} %pad_add_fusion.1.numbers, bf16[16,2,4,8,256]{4,3,2,1,0:T(8,128)(2,1)S(1)} %all-to-all-done.own, bf16[16,2,4,8,256]{4,3,2,1,0:T(8,128)(2,1)S(1)} %collective-permute-done.2.other, ...), custom_call_target="tpu_custom_call" | custom-call | tf_op jit(solution)/shard_map/angles/pallas_call | solution.py:198
  32.2 0.5 collective-permute-start.3
  32.7 1.9 %collective-permute-done.3 = bf16[4,4,4,24,256]{4,3,2,1,0:T(8,128)(2,1)S(1)} collective-permute-done((bf16[4,4,4,24,256]{4,3,2,1,0:T(8,128)(2,1)S(1)}, bf16[4,4,4,24,256]{4,3,2,1,0:T(8,128)(2,1)S(1)}, u32[]{:S(2)}, u32[]{:S(2)}) %collective-permute-start.3) | collective-permute-done | bytes 786464 | tf_op jit(solution)/shard_map/ppermute | solution.py:28
  34.6 0.2 add_convert_fusion
  34.9 19.2 %all_to_all.15 = bf16[16,4,24,256]{3,2,1,0:T(8,128)(2,1)S(1)} all-to-all(bf16[16,4,24,256]{3,2,1,0:T(8,128)(2,1)S(1)} %bitcast.39), channel_id=1, replica_groups=mesh['y'=4,'zh'=2,'zl'=4,'x'=4,'c'=2] {'y','x'}, dimensions={0} | all-to-all | bytes 1572864 | tf_op jit(solution)/shard_map/all_to_all | solution.py:32
  54.0 0.1 reduce_sum.12
  54.2 17.6 %all_to_all.16.column = bf16[32,24,256]{2,1,0:T(8,128)(2,1)S(1)} all-to-all(bf16[32,24,256]{2,1,0:T(8,128)(2,1)S(1)} %bitcast.40), channel_id=1, replica_groups=mesh['y'=4,'zh'=2,'zl'=4,'x'=4,'c'=2] {'y','zh','zl'}, dimensions={0} | all-to-all | bytes 786432 | tf_op jit(solution)/shard_map/all_to_all | solution.py:32
  71.8 1.2 %regularize.1 = (f32[2,4,8,256]{3,2,1,0:T(8,128)S(1)}, f32[2,4,8,256]{3,2,1,0:T(8,128)S(1)}) custom-call(s32[6]{0:T(128)S(1)} %pad_add_fusion.1.numbers, bf16[32,24,256]{2,1,0:T(8,128)(2,1)S(1)} %all_to_all.16.column, f32[4,24,256]{2,1,0:T(8,128)S(1)} %pad_maximum_fusion.params), custom_call_target="tpu_custom_call" | custom-call | tf_op jit(solution)/shard_map/regularize/pallas_call | solution.py:261
  73.0 4.9 %collective-permute-start.4 = (f32[2,4,8,256]{3,2,1,0:T(8,128)S(1)}, f32[2,4,8,256]{3,2,1,0:T(8,128)S(1)}, u32[]{:S(2)}, u32[]{:S(2)}) collective-permute-start(f32[2,4,8,256]{3,2,1,0:T(8,128)S(1)} %get-tuple-element.35), channel_id=1, source_target_pairs={{0,1},{1,0},{2,3},{3,2},{4,5},{5,4},{6,7},{7,6},{8,9},{9,8},{10,11... | collective-permute-start | bytes 196616 | tf_op jit(solution)/shard_map/ppermute | solution.py:28
  77.9 0.9 %collective-permute-done.4 = f32[2,4,8,256]{3,2,1,0:T(8,128)S(1)} collective-permute-done((f32[2,4,8,256]{3,2,1,0:T(8,128)S(1)}, f32[2,4,8,256]{3,2,1,0:T(8,128)S(1)}, u32[]{:S(2)}, u32[]{:S(2)}) %collective-permute-start.4) | collective-permute-done | bytes 65568 | tf_op jit(solution)/shard_map/ppermute | solution.py:28
  78.8 0.7 fusion.3
  (18 shorter events, 0.3 us)
Async XLA Ops:
  0.6 10.9 %copy-start.1 = (s32[2,2]{1,0:T(2,128)S(1)}, s32[2,2]{1,0:T(2,128)}, u32[]{:S(2)}) copy-start(s32[2,2]{1,0:T(2,128)} %tilts) | copy-start | bytes 52
  0.6 18.1 %copy-start.2 = (s32[2]{0:T(128)S(1)}, s32[2]{0:T(128)}, u32[]{:S(2)}) copy-start(s32[2]{0:T(128)} %param.10) | copy-start | bytes 28
  0.7 18.1 %copy-start.3 = (s32[2]{0:T(128)S(1)}, s32[2]{0:T(128)}, u32[]{:S(2)}) copy-start(s32[2]{0:T(128)} %param.9) | copy-start | bytes 28
  2.4 27.1 %copy-start = (bf16[2,2,256,256]{3,2,1,0:T(8,128)(2,1)S(1)}, bf16[2,2,256,256]{3,2,1,0:T(8,128)(2,1)}, u32[]{:S(2)}) copy-start(bf16[2,2,256,256]{3,2,1,0:T(8,128)(2,1)} %measured.1) | copy-start | bytes 1572868
  2.4 22.9 %all-to-all-start = ((bf16[16,2,4,8,256]{4,3,2,1,0:T(8,128)(2,1)}), bf16[16,2,4,8,256]{4,3,2,1,0:T(8,128)(2,1)S(1)}, u32[]{:S(2)}, u32[]{:S(2)}) async-start(bf16[16,2,4,8,256]{4,3,2,1,0:T(8,128)(2,1)} %transmission.1), calls=%async_computation | async-start | bytes 1048576 | tf_op jit(solution)/shard_map/all_to_all | solution.py:32
  14.3 6.9 %collective-permute-start = (f32[2,4,8,256]{3,2,1,0:T(8,128)S(1)}, f32[2,4,8,256]{3,2,1,0:T(8,128)S(1)}, u32[]{:S(2)}, u32[]{:S(2)}) collective-permute-start(f32[2,4,8,256]{3,2,1,0:T(8,128)S(1)} %pad_maximum_fusion.3.params), channel_id=1, source_target_pairs={{1,2},{3,4},{5,6},{7,8},{9,10},{11,12},{13,14},{15,16},{17,18},{19... | collective-permute-start | bytes 196616 | tf_op jit(solution)/shard_map/ppermute | solution.py:287
  21.2 1.3 %collective-permute-start.1 = (f32[2,4,8,256]{3,2,1,0:T(8,128)S(1)}, f32[2,4,8,256]{3,2,1,0:T(8,128)S(1)}, u32[]{:S(2)}, u32[]{:S(2)}) collective-permute-start(f32[2,4,8,256]{3,2,1,0:T(8,128)S(1)} %select_bitcast_fusion.2), channel_id=1, source_target_pairs={{0,1},{1,0},{2,3},{3,2},{4,5},{5,4},{6,7},{7,6},{8,9},{9,8},{10,11... | collective-permute-start | bytes 196616 | tf_op jit(solution)/shard_map/ppermute | solution.py:28
  25.3 4.2 %collective-permute-start.2 = (bf16[16,2,4,8,256]{4,3,2,1,0:T(8,128)(2,1)S(1)}, bf16[16,2,4,8,256]{4,3,2,1,0:T(8,128)(2,1)S(1)}, u32[]{:S(2)}, u32[]{:S(2)}) collective-permute-start(bf16[16,2,4,8,256]{4,3,2,1,0:T(8,128)(2,1)S(1)} %all-to-all-done.own), channel_id=1, source_target_pairs={{0,1},{1,0},{2,3},{3,2},{4,5},{5,4},{6,7},{7,6},{8,9},{9,8},{10,11... | collective-permute-start | bytes 1572872 | tf_op jit(solution)/shard_map/ppermute | solution.py:28
  32.2 2.4 %collective-permute-start.3 = (bf16[4,4,4,24,256]{4,3,2,1,0:T(8,128)(2,1)S(1)}, bf16[4,4,4,24,256]{4,3,2,1,0:T(8,128)(2,1)S(1)}, u32[]{:S(2)}, u32[]{:S(2)}) collective-permute-start(bf16[4,4,4,24,256]{4,3,2,1,0:T(8,128)(2,1)S(1)} %get-tuple-element.32), channel_id=1, source_target_pairs={{0,1},{1,0},{2,3},{3,2},{4,5},{5,4},{6,7},{7,6},{8,9},{9,8},{10,11... | collective-permute-start | bytes 2359304 | tf_op jit(solution)/shard_map/ppermute | solution.py:28
  73.0 5.8 %collective-permute-start.4 = (f32[2,4,8,256]{3,2,1,0:T(8,128)S(1)}, f32[2,4,8,256]{3,2,1,0:T(8,128)S(1)}, u32[]{:S(2)}, u32[]{:S(2)}) collective-permute-start(f32[2,4,8,256]{3,2,1,0:T(8,128)S(1)} %get-tuple-element.35), channel_id=1, source_target_pairs={{0,1},{1,0},{2,3},{3,2},{4,5},{5,4},{6,7},{7,6},{8,9},{9,8},{10,11... | collective-permute-start | bytes 196616 | tf_op jit(solution)/shard_map/ppermute | solution.py:28
